TPU v7x, 32 devices: a whole 2x2x4 slice. The times are simulated.
32 devices in a mesh: gx: 8 (over y, x, core), gy: 4 (over z).
Axes of the slice: x: 2, y: 2, z: 4, core: 2. Of those that a mesh axis runs over, the one named last changes fastest.
Arguments:
- potential: float32 [64, 1024, 256], P('gx', 'gy'), may hold values from -6 to 6
- classes: int32 [64, 1024, 256], P('gx', 'gy'), may hold values from 0 to 7
- sigma_table: float32 [8], replicated, may hold values from 0.5 to 5
- row_index: int32 [2], replicated, may hold values from 0 to 63
- col_index: int32 [2], replicated, may hold values from 0 to 1023
- depth_index: int32 [2], replicated, may hold values from 0 to 255
- currents: float32 [2], replicated, may hold values from -60 to 60
Outputs:
- new_potential: float32 [64, 1024, 256], P('gx', 'gy')
All inputs are finite; a program needn't handle non-finite values.
Results may differ from a plain program's by a relative error of at most 0.0003.
Values sent between devices are 32-bit elements; how exact they have to be, the bound alone decides.
No kernel may reach another device: no remote copies, remote signals or barrier semaphores. Data moves between devices by JAX's collectives and lax.ppermute only.
A program may use at most 128 MiB of HBM per device.

v0:
```python
import functools

import jax
import jax.numpy as jnp
from jax import lax
from jax.experimental import pallas as pl
from jax.experimental.pallas import tpu as pltpu
from jax.sharding import PartitionSpec as P

OMEGA = 0.8
HALO = 16
PAD = 8
LANES = 128
CHUNK = 32
F32 = jnp.float32
XL, XU, YL, YU, ZL, ZU = range(6)

VM = pl.BlockSpec(memory_space=pltpu.VMEM)
SM = pl.BlockSpec(memory_space=pltpu.SMEM)


class Dims:
    def __init__(self, shape):
        self.rows, self.cols, self.depth = shape
        self.halves = self.depth // LANES
        self.ext = self.cols + 2 * HALO
        self.padded = self.ext + 2 * PAD
        self.crows = self.rows // 2
        self.cext = self.ext // 2


def chunks(total, size, fn):
    def step(i, carry):
        fn(pl.multiple_of(i * size, 8))
        return carry

    lax.fori_loop(0, total // size, step, 0)


def lanes_of(rows):
    return lax.broadcasted_iota(jnp.int32, (rows, LANES), 1)


def below(parts):
    rolled = [pltpu.roll(part, 1, 1) for part in parts]
    first = lanes_of(parts[0].shape[0]) == 0
    return [rolled[0]] + [
        jnp.where(first, rolled[h - 1], rolled[h]) for h in range(1, len(parts))
    ]


def above(parts):
    rolled = [pltpu.roll(part, LANES - 1, 1) for part in parts]
    last = lanes_of(parts[0].shape[0]) == LANES - 1
    return [
        jnp.where(last, rolled[h + 1], rolled[h]) for h in range(len(parts) - 1)
    ] + [rolled[-1]]


def face(total):
    return jnp.where(total > 0, 2.0 / total, 0.0)


def lookup(cells, table):
    bits = [(cells & (1 << b)) != 0 for b in range(3)]
    level = [table[k] for k in range(8)]
    for bit in bits:
        level = [jnp.where(bit, level[k + 1], level[k]) for k in range(0, len(level), 2)]
    return level[0]


def sweep(dims, below_row, row, above_row, weights, out, scale=None, total=None):
    def body(y0):
        here = [row[h, pl.ds(y0 + PAD, CHUNK), :] for h in range(dims.halves)]
        zlow, zhigh = below(here), above(here)
        for h in range(dims.halves):
            span, wide = pl.ds(y0, CHUNK), pl.ds(y0 + PAD, CHUNK)
            acc = weights[XL][h, span, :] * below_row[h, wide, :]
            acc += weights[XU][h, span, :] * above_row[h, wide, :]
            acc += weights[YL][h, span, :] * row[h, pl.ds(y0 + PAD - 1, CHUNK), :]
            acc += weights[YU][h, span, :] * row[h, pl.ds(y0 + PAD + 1, CHUNK), :]
            acc += weights[ZL][h, span, :] * zlow[h]
            acc += weights[ZU][h, span, :] * zhigh[h]
            if scale is None:
                out[h, wide, :] = acc + (1.0 - OMEGA) * here[h]
            else:
                out[h, span, :] = (acc - OMEGA * here[h]) * scale[h, span, :]

    chunks(dims.ext, CHUNK, body)


def sources(dims, meta, cur, count, targets, fix):
    for s in range(count):
        row, col, dep = meta[s], meta[count + s], meta[2 * count + s]
        ext_col = col + HALO

        @pl.when(
            (row >= targets[0]) & (row <= targets[-1]) & (ext_col >= 0) & (ext_col < dims.ext)
        )
        def _():
            for x in targets:

                @pl.when(row == x)
                def _(x=x):
                    for h in range(dims.halves):
                        hit = lanes_of(1) == dep - h * LANES
                        fix(x, ext_col, h, jnp.where(hit, cur[s], 0.0))


def add_swept(field, scale, col, h, amount):
    field[h, pl.ds(col + PAD, 1), :] += amount / scale[h, pl.ds(col, 1), :]


def row_faces(dims, row, row_below_faces, yl_out, zl_out, xl_out):
    def body(y0):
        here = [row[h, pl.ds(y0 + PAD, CHUNK), :] for h in range(dims.halves)]
        zlow = below(here)
        first = lanes_of(CHUNK) == 0
        zlow[0] = jnp.where(first, 0.0, zlow[0])
        for h in range(dims.halves):
            wide = pl.ds(y0 + PAD, CHUNK)
            if xl_out is not None:
                xl_out[h, pl.ds(y0, CHUNK), :] = face(here[h] + row_below_faces[h, wide, :])
            if yl_out is not None:
                yl_out[h, wide, :] = face(here[h] + row[h, pl.ds(y0 + PAD - 1, CHUNK), :])
                zl_out[h, pl.ds(y0, CHUNK), :] = face(here[h] + zlow[h])

    chunks(dims.ext, CHUNK, body)


def row_weights(dims, row, xl, xu, yl, zl, weights, scale):
    def body(y0):
        span, wide = pl.ds(y0, CHUNK), pl.ds(y0 + PAD, CHUNK)
        low = [zl[h, span, :] for h in range(dims.halves)]
        high = above(low)
        lane = lanes_of(CHUNK)
        top = dims.halves - 1
        high[top] = jnp.where(lane == LANES - 1, face(row[top, wide, :]), high[top])
        for h in range(dims.halves):
            parts = [
                xl[h, span, :],
                xu[h, span, :],
                yl[h, wide, :],
                yl[h, pl.ds(y0 + PAD + 1, CHUNK), :],
                low[h],
                high[h],
            ]
            diag = parts[0] + parts[1] + parts[2] + parts[3] + parts[4] + parts[5]
            gain = jnp.where(row[h, wide, :] > 0, OMEGA / diag, 0.0)
            scale[h, span, :] = diag * (1.0 / OMEGA)
            if h == 0:
                parts[ZL] = jnp.where(lane == 0, 0.0, parts[ZL])
            if h == top:
                parts[ZU] = jnp.where(lane == LANES - 1, 0.0, parts[ZU])
            for k in range(6):
                weights[k][h, span, :] = gain * parts[k]

    chunks(dims.ext, CHUNK, body)


def split_dot(field, chosen):
    total = None
    for _ in range(3):
        piece = field.astype(jnp.bfloat16)
        field = field - piece.astype(F32)
        term = jnp.dot(piece, chosen, preferred_element_type=F32)
        total = term if total is None else total + term
    return total


def picker(dims, h, lowest, highest):
    fine = lax.broadcasted_iota(jnp.int32, (LANES, LANES), 0) + h * LANES
    coarse = lax.broadcasted_iota(jnp.int32, (LANES, LANES), 1)
    hit = (fine >= 2 * coarse + lowest) & (fine <= 2 * coarse + highest)
    return jnp.where(hit, 1.0, 0.0).astype(jnp.bfloat16)


def restrict(dims, rows, offset, parities, chosen):
    total = None
    for h in range(dims.halves):
        acc = None
        for row in rows:
            for parity in parities:
                part = row[h, pl.ds(offset + parity, dims.cext, stride=2), :]
                acc = part if acc is None else acc + part
        term = split_dot(acc, chosen[h])
        total = term if total is None else total + term
    return total


def first_kernel(dims, nsrc, meta, cur, table, pot, cls, yod, yev, *refs):
    (wts, scl, one, two, rsd, eres, evol, efx, efy, efz, cfc, ins, send_od, send_ev) = refs[:14]
    res, vol, fx, fy, fz = refs[14:]
    rows, halves, cols = dims.rows, dims.halves, dims.cols
    odd_x, odd_y = meta[3 * nsrc] == 1, meta[3 * nsrc + 1] == 1
    lanes = [slice(h * LANES, (h + 1) * LANES) for h in range(halves)]

    def halo_res(code):
        number = code.astype(jnp.int32)
        return jnp.where(number > 0, lookup(number - 1, table), 0.0)

    def assemble(x, carry):
        for h in range(halves):
            zero = jnp.zeros((PAD, LANES), F32)
            for ref in (res, vol):
                ref[x, h, pl.ds(0, PAD), :] = zero
                ref[x, h, pl.ds(PAD + dims.ext, PAD), :] = zero
            for into, take_ev in ((PAD, True), (PAD + HALO + cols, False)):
                pair = []
                for k in range(2):
                    a, b = yod[k, x, :, lanes[h]], yev[k, x, :, lanes[h]]
                    pair.append(jnp.where(odd_y, b, a) if take_ev else jnp.where(odd_y, a, b))
                vol[x, h, pl.ds(into, HALO), :] = pair[0]
                res[x, h, pl.ds(into, HALO), :] = halo_res(pair[1])

            def own(y0):
                vol[x, h, pl.ds(y0 + PAD + HALO, CHUNK), :] = pot[x, pl.ds(y0, CHUNK), lanes[h]]
                res[x, h, pl.ds(y0 + PAD + HALO, CHUNK), :] = lookup(
                    cls[x, pl.ds(y0, CHUNK), lanes[h]], table
                )

            chunks(cols, CHUNK, own)
        return carry

    lax.fori_loop(0, rows, assemble, 0)

    for x in range(rows):
        for h in range(halves):
            fy[x, h, pl.ds(PAD + dims.ext, PAD), :] = jnp.zeros((PAD, LANES), F32)
        row_faces(
            dims,
            res.at[x],
            res.at[x - 1] if x else None,
            fy.at[x],
            fz.at[x],
            fx.at[x] if x else None,
        )
    for x in range(1, rows - 1):
        row_weights(
            dims,
            res.at[x],
            fx.at[x],
            fx.at[x + 1],
            fy.at[x],
            fz.at[x],
            [wts.at[k, x - 1] for k in range(6)],
            scl.at[x - 1],
        )
    weights = lambda x: [wts.at[k, x - 1] for k in range(6)]

    for x in range(1, rows - 1):
        sweep(dims, vol.at[x - 1], vol.at[x], vol.at[x + 1], weights(x), one.at[x - 1])

    sources(
        dims, meta, cur, nsrc, range(1, rows - 1),
        lambda x, *rest: add_swept(one.at[x - 1], scl.at[x - 1], *rest),
    )

    def fill(send, high):
        edge = jnp.where(high, rows - 2, 0)
        inner = jnp.where(high, rows - 2, 1)
        for h in range(halves):
            send[pl.ds(h * dims.ext, dims.ext), :] = one[inner - 1, h, pl.ds(PAD, dims.ext), :]
        base = halves * dims.ext
        for k in range(4):
            ref = vol if k < 2 else res
            for h in range(halves):
                at = base + (k * halves + h) * 2 * HALO
                send[pl.ds(at, HALO), :] = ref[edge + k % 2, h, pl.ds(PAD, HALO), :]
                send[pl.ds(at + HALO, HALO), :] = ref[
                    edge + k % 2, h, pl.ds(PAD + HALO + cols, HALO), :
                ]

    fill(send_od, odd_x)
    fill(send_ev, jnp.logical_not(odd_x))

    for x in range(2, rows - 2):
        sweep(dims, one.at[x - 2], one.at[x - 1], one.at[x], weights(x), two.at[x - 2])

    sources(
        dims, meta, cur, nsrc, range(2, rows - 2),
        lambda x, *rest: add_swept(two.at[x - 2], scl.at[x - 1], *rest),
    )

    for x in range(3, rows - 3):
        sweep(
            dims, two.at[x - 3], two.at[x - 2], two.at[x - 1], weights(x), rsd.at[x - 3],
            scl.at[x - 1],
        )

    def fix_rsd(row, col, h, amount):
        rsd[row - 3, h, pl.ds(col, 1), :] += amount

    sources(dims, meta, cur, nsrc, range(3, rows - 3), fix_rsd)

    def keep(y0):
        span, wide = pl.ds(y0, CHUNK), pl.ds(y0 + PAD, CHUNK)
        for h in range(halves):
            for k, x in enumerate((0, rows - 1)):
                eres[k, h, wide, :] = res[x, h, wide, :]
                efy[k, h, wide, :] = fy[x, h, wide, :]
                efz[k, h, span, :] = fz[x, h, span, :]
            for k, x in enumerate((0, 1, rows - 2, rows - 1)):
                evol[k, h, wide, :] = vol[x, h, wide, :]
            for k, x in enumerate((1, rows - 1)):
                efx[k, h, span, :] = fx[x, h, span, :]

    chunks(dims.ext, CHUNK, keep)
    for h in range(halves):
        zeros = jnp.zeros((PAD, LANES), F32)
        for ref, count in ((eres, 2), (efy, 2), (evol, 4)):
            for k in range(count):
                ref[k, h, pl.ds(0, PAD), :] = zeros
                ref[k, h, pl.ds(PAD + dims.ext, PAD), :] = zeros

    both = [picker(dims, h, 0, 1) for h in range(halves)]
    even = [picker(dims, h, 0, 0) for h in range(halves)]
    n = dims.crows
    for c in range(n):
        pair = lambda ref: [ref.at[2 * c], ref.at[2 * c + 1]]
        if c:
            cfc[c] = restrict(dims, [fx.at[2 * c]], 0, (0, 1), both)
        cfc[n + 1 + c] = restrict(dims, pair(fy), PAD, (0,), both)
        cfc[2 * n + 1 + c] = restrict(dims, pair(fz), 0, (0, 1), even)
        top = None
        for row in pair(res):
            for parity in (0, 1):
                part = face(row[halves - 1, pl.ds(PAD + parity, dims.cext, stride=2), :])
                top = part if top is None else top + part
        cfc[3 * n + 1 + c] = top
        ins[c] = res[2 * c, 0, pl.ds(PAD, dims.cext, stride=2), :]


def neighbours(rows):
    ext = rows.shape[0]
    return (
        pltpu.roll(rows, 1, 0),
        pltpu.roll(rows, ext - 1, 0),
        pltpu.roll(rows, 1, 1),
        pltpu.roll(rows, LANES - 1, 1),
    )


def coarse_side(field, base, weights):
    ylow, yhigh, zlow, zhigh = neighbours(field)
    return (
        (1.0 - OMEGA) * field
        + base
        + weights[YL] * ylow
        + weights[YU] * yhigh
        + weights[ZL] * zlow
        + weights[ZU] * zhigh
    )


def second_kernel(dims, nsrc, meta, cur, table, xod, xev, sod, sev, wts, scl, one, two, rsd, res,
                  vol, fx, fy, fz, cfc, ins, hwts, hscl, htwo, gco, base, c_od, c_ev, v_od, v_ev,
                  hres, hvol, hfx, hfy, hfz, edge, redge):
    rows, halves, cols = dims.rows, dims.halves, dims.cols
    odd_x = meta[3 * nsrc] == 1
    lanes = [slice(h * LANES, (h + 1) * LANES) for h in range(halves)]
    last = rows - 1

    def halo_res(code):
        number = code.astype(jnp.int32)
        return jnp.where(number > 0, lookup(number - 1, table), 0.0)

    for side in range(2):
        choose = lambda a, b: jnp.where(odd_x, b, a) if side == 0 else jnp.where(odd_x, a, b)
        for k in range(2):
            at = 2 * side + k
            for h in range(halves):
                zero = jnp.zeros((PAD, LANES), F32)
                for ref in (hres, hvol):
                    ref[at, h, pl.ds(0, PAD), :] = zero
                    ref[at, h, pl.ds(PAD + dims.ext, PAD), :] = zero
                for ref, kind in ((hvol, k), (hres, 2 + k)):
                    strip = halves * dims.ext + (kind * halves + h) * 2 * HALO
                    low = pl.ds(strip, HALO)
                    high = pl.ds(strip + HALO, HALO)
                    ref[at, h, pl.ds(PAD, HALO), :] = choose(sod[low, :], sev[low, :])
                    ref[at, h, pl.ds(PAD + HALO + cols, HALO), :] = choose(
                        sod[high, :], sev[high, :]
                    )

                def own(y0):
                    span = pl.ds(y0, CHUNK)
                    wide = pl.ds(y0 + PAD + HALO, CHUNK)
                    hvol[at, h, wide, :] = choose(xod[k, span, lanes[h]], xev[k, span, lanes[h]])
                    hres[at, h, wide, :] = halo_res(
                        choose(xod[2 + k, span, lanes[h]], xev[2 + k, span, lanes[h]])
                    )

                chunks(cols, CHUNK, own)
        for h in range(halves):

            def swept(y0):
                span = pl.ds(h * dims.ext + y0, CHUNK)
                edge[5 * side, h, pl.ds(y0 + PAD, CHUNK), :] = choose(sod[span, :], sev[span, :])

            chunks(dims.ext, CHUNK, swept)

    row_faces(dims, hres.at[1], hres.at[0], hfy.at[0], hfz.at[0], hfx.at[0])
    row_faces(dims, res.at[0], hres.at[1], None, None, hfx.at[1])
    row_faces(dims, hres.at[2], res.at[1], hfy.at[1], hfz.at[1], hfx.at[2])
    row_faces(dims, hres.at[3], hres.at[2], None, None, hfx.at[3])
    for side in range(2):
        for h in range(halves):
            hfy[side, h, pl.ds(PAD + dims.ext, PAD), :] = jnp.zeros((PAD, LANES), F32)

    outer = lambda x: x + 1 if x <= 0 else x - last + 2
    inner = lambda x: 1 <= x <= last - 1
    weights = lambda x: [
        wts.at[k, x - 1] if inner(x) else hwts.at[k, outer(x)] for k in range(6)
    ]
    scale = lambda x: scl.at[x - 1] if inner(x) else hscl.at[outer(x)]
    for x, row, xl, xu, yl, zl in (
        (-1, hres.at[1], hfx.at[0], hfx.at[1], hfy.at[0], hfz.at[0]),
        (0, res.at[0], hfx.at[1], fx.at[0], fy.at[0], fz.at[0]),
        (last, res.at[1], fx.at[1], hfx.at[2], fy.at[1], fz.at[1]),
        (rows, hres.at[2], hfx.at[2], hfx.at[3], hfy.at[1], hfz.at[1]),
    ):
        row_weights(dims, row, xl, xu, yl, zl, weights(x), scale(x))

    def start(x):
        if x < 0:
            return hvol.at[x + 2]
        if x >= rows:
            return hvol.at[x - rows + 2]
        return vol.at[x if x <= 1 else x - last + 3]

    def swept(x):
        if x <= 0:
            return edge.at[x + 2]
        return one.at[x - 1] if x < last else edge.at[x - last + 3]

    for x in (-1, 0, last, rows):
        sweep(dims, start(x - 1), start(x), start(x + 1), weights(x), swept(x))

    sources(
        dims, meta, cur, nsrc, (-1, 0, last, rows),
        lambda x, *rest: add_swept(swept(x), scale(x), *rest),
    )

    def twice(x):
        if x <= 1:
            return htwo.at[x + 1]
        return two.at[x - 2] if x < last - 1 else htwo.at[x - last + 4]

    for x in (-1, 0, 1, last - 1, last, rows):
        sweep(dims, swept(x - 1), swept(x), swept(x + 1), weights(x), twice(x))
    sources(
        dims, meta, cur, nsrc, (-1, 0, 1, last - 1, last, rows),
        lambda x, *rest: add_swept(twice(x), scale(x), *rest),
    )

    def resid_row(x):
        if x <= 2:
            return redge.at[x]
        return rsd.at[x - 3] if x < last - 2 else redge.at[x - last + 5]

    for x in (0, 1, 2, last - 2, last - 1, last):
        sweep(
            dims, twice(x - 1), twice(x), twice(x + 1), weights(x), resid_row(x), scale(x)
        )

    def fix_rsd(x, col, h, amount):
        resid_row(x)[h, pl.ds(col, 1), :] += amount

    sources(dims, meta, cur, nsrc, (0, 1, 2, last - 2, last - 1, last), fix_rsd)

    both = [picker(dims, h, 0, 1) for h in range(halves)]
    n = dims.crows
    lane = lanes_of(dims.cext)
    bottom = restrict(dims, [hfx.at[1]], 0, (0, 1), both)
    topmost = restrict(dims, [hfx.at[2]], 0, (0, 1), both)

    e1, gc = [], []
    for c in range(n):
        xl = bottom if c == 0 else cfc[c]
        xu = topmost if c == n - 1 else cfc[c + 1]
        yl, zl = cfc[n + 1 + c], cfc[2 * n + 1 + c]
        yu = pltpu.roll(yl, dims.cext - 1, 0)
        zu = jnp.where(lane == LANES - 1, cfc[3 * n + 1 + c], pltpu.roll(zl, LANES - 1, 1))
        diag = xl + xu + yl + yu + zl + zu
        inside = ins[c] > 0
        gain = jnp.where(inside, OMEGA / diag, 0.0)
        zl = jnp.where(lane == 0, 0.0, zl)
        zu = jnp.where(lane == LANES - 1, 0.0, zu)
        gc.append([gain * part for part in (xl, xu, yl, yu, zl, zu)])
        for k in range(6):
            gco[k, c] = gc[c][k]
        total = restrict(dims, [resid_row(2 * c), resid_row(2 * c + 1)], 0, (0, 1), both)
        e1.append(gain * total)
        base[c] = e1[c]

    low = (e1[0], coarse_side(e1[0], e1[0], gc[0]) + gc[0][XU] * e1[1], gc[0][XL])
    high = (
        e1[n - 1],
        coarse_side(e1[n - 1], e1[n - 1], gc[n - 1]) + gc[n - 1][XL] * e1[n - 2],
        gc[n - 1][XU],
    )
    for k in range(3):
        c_od[k] = jnp.where(odd_x, high[k], low[k])
        c_ev[k] = jnp.where(odd_x, low[k], high[k])
    pick_od = jnp.where(odd_x, 3, 2)
    pick_ev = jnp.where(odd_x, 2, 3)
    for h in range(halves):

        def out(y0):
            wide = pl.ds(y0 + PAD, CHUNK)
            v_od[h, pl.ds(y0, CHUNK), :] = htwo[pick_od, h, wide, :]
            v_ev[h, pl.ds(y0, CHUNK), :] = htwo[pick_ev, h, wide, :]

        chunks(dims.ext, CHUNK, out)


def third_kernel(dims, nsrc, meta, gco, base, rod, rev, e3, c_od, c_ev):
    n = dims.crows
    odd_x = meta[3 * nsrc] == 1
    low = [jnp.where(odd_x, rev[k], rod[k]) for k in range(3)]
    high = [jnp.where(odd_x, rod[k], rev[k]) for k in range(3)]
    gc = lambda c: [gco[k, c] for k in range(6)]

    def coarse_sweep(field, under, over):
        out = []
        for c in range(n):
            w = gc(c)
            new = coarse_side(field[c], base[c], w)
            new += w[XL] * (field[c - 1] if c else under)
            new += w[XU] * (field[c + 1] if c < n - 1 else over)
            out.append(new)
        return out

    e1 = [base[c] for c in range(n)]
    e2 = coarse_sweep(e1, low[0], high[0])
    under = low[1] + low[2] * e1[0]
    over = high[1] + high[2] * e1[n - 1]
    out = coarse_sweep(e2, under, over)
    for c in range(n):
        e3[c] = out[c]
    w = gc(0)
    first = (out[0], coarse_side(out[0], base[0], w) + w[XU] * out[1])
    w = gc(n - 1)
    final = (out[n - 1], coarse_side(out[n - 1], base[n - 1], w) + w[XL] * out[n - 2])
    for k in range(2):
        c_od[k] = jnp.where(odd_x, final[k], first[k])
        c_ev[k] = jnp.where(odd_x, first[k], final[k])


def fourth_kernel(dims, nsrc, meta, cur, gco, base, e3, rod, rev, tod, tev, vod, vev, wts, scl, two,
                  hwts, hscl, htwo, out, raised, zero, three, done, sems):
    rows, halves, cols = dims.rows, dims.halves, dims.cols
    n = dims.crows
    odd_x = meta[3 * nsrc] == 1
    below_of = lambda od, ev: jnp.where(odd_x, ev, od)
    above_of = lambda od, ev: jnp.where(odd_x, od, ev)
    field = [e3[c] for c in range(n)]
    under = below_of(tod[1], tev[1]) + below_of(rod[2], rev[2]) * field[0]
    over = above_of(tod[1], tev[1]) + above_of(rod[2], rev[2]) * field[n - 1]
    e4 = [under]
    for c in range(n):
        w = [gco[k, c] for k in range(6)]
        new = coarse_side(field[c], base[c], w)
        new += w[XL] * (field[c - 1] if c else below_of(tod[0], tev[0]))
        new += w[XU] * (field[c + 1] if c < n - 1 else above_of(tod[0], tev[0]))
        e4.append(new)
    e4.append(over)
    spread = []
    for h in range(halves):
        fine = lax.broadcasted_iota(jnp.int32, (LANES, LANES), 1) + h * LANES
        coarse = lax.broadcasted_iota(jnp.int32, (LANES, LANES), 0)
        hit = (fine >= 2 * coarse) & (fine <= 2 * coarse + 1)
        spread.append(jnp.where(hit, 1.0, 0.0).astype(jnp.bfloat16))
    for c in range(n + 2):
        for h in range(halves):
            lifted = split_dot(e4[c], spread[h])
            raised[c, h, pl.ds(0, dims.cext, stride=2), :] = lifted
            raised[c, h, pl.ds(1, dims.cext, stride=2), :] = lifted

    last = rows - 1

    def twice(x):
        if x <= 1:
            return htwo.at[x + 1]
        return two.at[x - 2] if x < last - 1 else htwo.at[x - last + 4]

    outer = lambda x: x + 1 if x <= 0 else x - last + 2
    inner = lambda x: 1 <= x <= last - 1
    weights = lambda x: [
        wts.at[k, x - 1] if inner(x) else hwts.at[k, outer(x)] for k in range(6)
    ]
    scale = lambda x: scl.at[x - 1] if inner(x) else hscl.at[outer(x)]
    for x in range(-2, rows + 2):
        for h in range(halves):

            def add(y0):
                span, wide = pl.ds(y0, CHUNK), pl.ds(y0 + PAD, CHUNK)
                if x == -2:
                    value = below_of(vod[h, span, :], vev[h, span, :])
                elif x == rows + 1:
                    value = above_of(vod[h, span, :], vev[h, span, :])
                else:
                    value = twice(x)[h, wide, :]
                zero[x + 2, h, wide, :] = value + raised[(x + 2) // 2, h, span, :]

            chunks(dims.ext, CHUNK, add)

    for x in range(-1, rows + 1):
        sweep(dims, zero.at[x + 1], zero.at[x + 2], zero.at[x + 3], weights(x), three.at[x + 1])

    sources(
        dims, meta, cur, nsrc, range(-1, rows + 1),
        lambda x, *rest: add_swept(three.at[x + 1], scale(x), *rest),
    )

    copies = []
    for x in range(rows):
        below_row, row, above_row = three.at[x], three.at[x + 1], three.at[x + 2]
        w = weights(x)

        def body(y0):
            at = y0 + PAD + HALO
            here = [row[h, pl.ds(at, CHUNK), :] for h in range(halves)]
            zlow, zhigh = below(here), above(here)
            for h in range(halves):
                span = pl.ds(y0 + HALO, CHUNK)
                acc = w[XL][h, span, :] * below_row[h, pl.ds(at, CHUNK), :]
                acc += w[XU][h, span, :] * above_row[h, pl.ds(at, CHUNK), :]
                acc += w[YL][h, span, :] * row[h, pl.ds(at - 1, CHUNK), :]
                acc += w[YU][h, span, :] * row[h, pl.ds(at + 1, CHUNK), :]
                acc += w[ZL][h, span, :] * zlow[h]
                acc += w[ZU][h, span, :] * zhigh[h]
                done[x, pl.ds(y0, CHUNK), h * LANES : (h + 1) * LANES] = (
                    acc + (1.0 - OMEGA) * here[h]
                )

        chunks(cols, CHUNK, body)

        for s in range(nsrc):
            r, col, dep = meta[s], meta[nsrc + s], meta[2 * nsrc + s]

            @pl.when((r == x) & (col >= 0) & (col < cols))
            def _():
                for h in range(halves):
                    block = pl.multiple_of(col // 8 * 8, 8)
                    place = lax.broadcasted_iota(jnp.int32, (8, LANES), 0) + block
                    hit = (lanes_of(8) == dep - h * LANES) & (place == col)
                    amount = jnp.where(hit, cur[s], 0.0)
                    done[x, pl.ds(block, 8), h * LANES : (h + 1) * LANES] += (
                        amount / scale(x)[h, pl.ds(block + HALO, 8), :]
                    )

        copy = pltpu.make_async_copy(done.at[x], out.at[x], sems.at[x])
        copy.start()
        copies.append(copy)
    for copy in copies:
        copy.wait()


def call(kernel, outs, ins, specs, scratch=(), aliases=None, out_specs=None, limit=24, cost=1):
    return pl.pallas_call(
        kernel,
        out_shape=[jax.ShapeDtypeStruct(shape, F32) for shape in outs],
        in_specs=specs,
        out_specs=out_specs if out_specs is not None else [VM] * len(outs),
        scratch_shapes=list(scratch),
        input_output_aliases=aliases or {},
        compiler_params=pltpu.CompilerParams(vmem_limit_bytes=limit * 2**20),
        cost_estimate=pl.CostEstimate(flops=cost, bytes_accessed=cost, transcendentals=0),
    )(*ins)


def swaps(count):
    pairs = []
    for first in (1, 0):
        found = []
        for low in range(first, count - 1, 2):
            found += [(low, low + 1), (low + 1, low)]
        pairs.append(found)
    return pairs


def swap(od, ev, axis):
    odd_pairs, even_pairs = swaps(lax.axis_size(axis))
    return lax.ppermute(od, axis, odd_pairs), lax.ppermute(ev, axis, even_pairs)


def per_device(potential, classes, sigma_table, row_index, col_index, depth_index, currents):
    dims = Dims(potential.shape)
    rows, cols, depth = potential.shape
    halves, ext, padded, n, cext = dims.halves, dims.ext, dims.padded, dims.crows, dims.cext
    nsrc = row_index.shape[0]
    gx, gy = lax.axis_index("gx"), lax.axis_index("gy")
    odd_x, odd_y = gx % 2, gy % 2
    meta = jnp.concatenate(
        [
            row_index - gx * rows,
            col_index - gy * cols,
            depth_index,
            jnp.stack([odd_x, odd_y]),
        ]
    ).astype(jnp.int32)
    table = 1.0 / sigma_table

    def edges(dim, width, high):
        start = jnp.where(high, potential.shape[dim] - width, 0)
        return [
            lax.dynamic_slice_in_dim(potential, start, width, dim),
            lax.dynamic_slice_in_dim(classes, start, width, dim).astype(F32) + 1.0,
        ]

    xod, xev = swap(
        jnp.concatenate(edges(0, 2, odd_x == 1)), jnp.concatenate(edges(0, 2, odd_x == 0)), "gx"
    )
    yod, yev = swap(
        jnp.stack(edges(1, HALO, odd_y == 1)), jnp.stack(edges(1, HALO, odd_y == 0)), "gy"
    )

    bind = lambda kernel: functools.partial(kernel, dims, nsrc)
    wide = lambda k: (k, halves, padded, LANES)
    flat = lambda k: (k, halves, ext, LANES)
    send = (halves * ext + 4 * halves * 2 * HALO, LANES)
    coarse = lambda *k: (*k, cext, LANES)
    (wts, scl, one, two, rsd, res, vol, fx, fy, fz, cfc, ins, sod, sev) = call(
        bind(first_kernel),
        [
            (6, *flat(rows - 2)), flat(rows - 2), wide(rows - 2), wide(rows - 4), flat(rows - 6),
            wide(2), wide(4), flat(2), wide(2), flat(2), coarse(4 * n + 1), coarse(n), send, send,
        ],
        [meta, currents, table, potential, classes, yod, yev],
        [SM, SM, SM, VM, VM, VM, VM],
        scratch=[pltpu.VMEM(shape, F32) for shape in (
            wide(rows), wide(rows), flat(rows), wide(rows), flat(rows))],
        limit=16,
    )
    sod, sev = swap(sod, sev, "gx")
    (hwts, hscl, htwo, gco, base, c_od, c_ev, v_od, v_ev) = call(
        bind(second_kernel),
        [
            (6, *flat(4)), flat(4), wide(6), coarse(6, n), coarse(n),
            coarse(3), coarse(3), flat(1)[1:], flat(1)[1:],
        ],
        [meta, currents, table, xod, xev, sod, sev, wts, scl, one, two, rsd, res, vol, fx, fy, fz,
         cfc, ins],
        [SM] * 3 + [VM] * 16,
        scratch=[pltpu.VMEM(shape, F32) for shape in (
            wide(4), wide(4), flat(4), wide(2), flat(2), wide(6), flat(6))],
        limit=16,
    )
    rod, rev = swap(c_od, c_ev, "gx")
    vod, vev = swap(v_od, v_ev, "gx")
    (e3, t_od, t_ev) = call(
        bind(third_kernel),
        [coarse(n), coarse(2), coarse(2)],
        [meta, gco, base, rod, rev],
        [SM] + [VM] * 4,
        limit=8,
    )
    tod, tev = swap(t_od, t_ev, "gx")
    (out,) = call(
        bind(fourth_kernel),
        [(rows, cols, depth)],
        [meta, currents, gco, base, e3, rod, rev, tod, tev, vod, vev, wts, scl, two, hwts, hscl,
         htwo],
        [SM] * 2 + [VM] * 15,
        scratch=[pltpu.VMEM(shape, F32) for shape in (
            flat(n + 2), wide(rows + 4), wide(rows + 2), (rows, cols, depth))]
        + [pltpu.SemaphoreType.DMA((rows,))],
        out_specs=[pl.BlockSpec(memory_space=pl.ANY)],
        limit=24,
    )
    return out


def solution(mesh):
    tiled = P("gx", "gy", None)
    return jax.shard_map(
        per_device,
        mesh=mesh,
        in_specs=(tiled, tiled, P(), P(), P(), P(), P()),
        out_specs=tiled,
        check_vma=False,
    )
```

profile of v0, /device:TPU:11, one launch (start us, length us, event | category | flops | bytes accessed | tf_op | source)
XLA Modules:
  0.0 127.5 jit_solution(4401841871293488642)
XLA Ops:
  0.0 1.7 %convert_add_fusion = (f32[2,256,256]{2,1,0:T(8,128)S(1)}, f32[2,256,256]{2,1,0:T(8,128)S(1)}, f32[2,256,256]{2,1,0:T(8,128)S(1)}, f32[2,256,256]{2,1,0:T(8,128)S(1)}) fusion(s32[8,256,256]{2,1,0:T(8,128)} %cls.1, s32[]{:T(128)S(6)} %select_n.35, s32[]{:T(128)S(6)} %select_n.34, f32[8,256,256]{2,1,0:T(8,128)} %pot.1), kind=kLoop, calls=%fused_computation.2 | loop fusion | flops 524288 | bytes 4194312 | tf_op jit(solution)/shard_map/add | solution.py:710
  1.7 0.0 copy-start.2
  1.7 1.0 pad_maximum_fusion
  2.7 3.7 %collective-permute-start = (f32[4,256,256]{2,1,0:T(8,128)}, f32[4,256,256]{2,1,0:T(8,128)S(1)}, u32[]{:S(2)}, u32[]{:S(2)}) collective-permute-start(f32[4,256,256]{2,1,0:T(8,128)} %pad_maximum_fusion), channel_id=1, source_target_pairs={{4,8},{8,4},{12,16},{16,12},{20,24},{24,20},{5,9},{9,5},{13,17},{1... | collective-permute-start | bytes 3145736 | tf_op jit(solution)/shard_map/ppermute | solution.py:686
  6.4 0.0 copy-start.5
  6.4 0.0 copy-start.6
  6.4 0.0 copy-start.7
  6.4 0.0 copy-start.8
  6.4 0.0 copy-start.4
  6.5 1.1 pad_maximum_fusion.1
  7.5 0.0 collective-permute-start.1
  7.5 0.0 copy-done.2
  7.5 1.0 add_bitcast_fusion
  8.6 0.7 pad_maximum_fusion.2
  9.3 3.2 %collective-permute-start.2 = (f32[2,8,16,256]{3,2,1,0:T(8,128)}, f32[2,8,16,256]{3,2,1,0:T(8,128)S(1)}, u32[]{:S(2)}, u32[]{:S(2)}) collective-permute-start(f32[2,8,16,256]{3,2,1,0:T(8,128)} %pad_maximum_fusion.2), channel_id=1, source_target_pairs={{1,2},{2,1},{5,6},{6,5},{9,10},{10,9},{13,14},{14,13},{17,18},{18,... | collective-permute-start | bytes 786440 | tf_op jit(solution)/shard_map/ppermute | solution.py:686
  12.5 0.7 pad_maximum_fusion.3
  13.2 0.0 collective-permute-start.3
  13.2 0.0 copy-done.5
  13.2 0.0 copy-done.6
  13.2 0.1 concatenate.9.meta
  13.3 5.5 %collective-permute-done.2.yod = f32[2,8,16,256]{3,2,1,0:T(8,128)S(1)} collective-permute-done((f32[2,8,16,256]{3,2,1,0:T(8,128)}, f32[2,8,16,256]{3,2,1,0:T(8,128)S(1)}, u32[]{:S(2)}, u32[]{:S(2)}) %collective-permute-start.2) | collective-permute-done | bytes 262176 | tf_op jit(solution)/shard_map/ppermute | solution.py:686
  18.8 1.7 %collective-permute-done.3.yev = f32[2,8,16,256]{3,2,1,0:T(8,128)} collective-permute-done((f32[2,8,16,256]{3,2,1,0:T(8,128)}, f32[2,8,16,256]{3,2,1,0:T(8,128)}, u32[]{:S(2)}, u32[]{:S(2)}) %collective-permute-start.3) | collective-permute-done | bytes 262176 | tf_op jit(solution)/shard_map/ppermute | solution.py:686
  20.6 1.6 %copy-done.3 = f32[8,256,256]{2,1,0:T(8,128)S(1)} copy-done((f32[8,256,256]{2,1,0:T(8,128)S(1)}, f32[8,256,256]{2,1,0:T(8,128)}, u32[]{:S(2)}) %copy-start.3) | copy-done | bytes 2097176
  22.2 26.2 %shard_map.73 = (f32[6,6,2,288,128]{4,3,2,1,0:T(8,128)S(1)}, f32[6,2,288,128]{3,2,1,0:T(8,128)S(1)}, f32[6,2,304,128]{3,2,1,0:T(8,128)S(1)}, f32[4,2,304,128]{3,...) custom-call(s32[8]{0:T(128)S(1)} %concatenate.9.meta, ...), custom_call_target="tpu_custom_call" | custom-call | flops 1 | bytes 1 | tf_op jit(solution)/shard_map/pallas_call | solution.py:662
  48.4 4.7 %collective-permute-start.4 = (f32[832,128]{1,0:T(8,128)S(1)}, f32[832,128]{1,0:T(8,128)S(1)}, u32[]{:S(2)}, u32[]{:S(2)}) collective-permute-start(f32[832,128]{1,0:T(8,128)S(1)} %get-tuple-element.31), channel_id=1, source_target_pairs={{4,8},{8,4},{12,16},{16,12},{20,24},{24,20},{5,9},{9,5},{13,17},{1... | collective-permute-start | bytes 1277960 | tf_op jit(solution)/shard_map/ppermute | solution.py:686
  53.1 0.1 collective-permute-start.5
  53.1 10.1 %collective-permute-done.4.sod = f32[832,128]{1,0:T(8,128)S(1)} collective-permute-done((f32[832,128]{1,0:T(8,128)S(1)}, f32[832,128]{1,0:T(8,128)S(1)}, u32[]{:S(2)}, u32[]{:S(2)}) %collective-permute-start.4) | collective-permute-done | bytes 426016 | tf_op jit(solution)/shard_map/ppermute | solution.py:686
  63.2 0.0 collective-permute-done.5.sev
  63.3 0.0 collective-permute-done.xod
  63.3 0.0 collective-permute-done.1.xev
  63.3 22.2 %shard_map.74 = (f32[6,4,2,288,128]{4,3,2,1,0:T(8,128)S(1)}, f32[4,2,288,128]{3,2,1,0:T(8,128)S(1)}, f32[6,2,304,128]{3,2,1,0:T(8,128)S(1)}, f32[6,4,144,128]{3,...) custom-call(s32[8]{0:T(128)S(1)} %concatenate.9.meta, ...), custom_call_target="tpu_custom_call" | custom-call | flops 1 | bytes 1 | tf_op jit(solution)/shard_map/pallas_call | solution.py:662
  85.5 0.0 copy-start
  85.5 2.8 %copy-done = f32[6,4,2,288,128]{4,3,2,1,0:T(8,128)} copy-done((f32[6,4,2,288,128]{4,3,2,1,0:T(8,128)}, f32[6,4,2,288,128]{4,3,2,1,0:T(8,128)S(1)}, u32[]{:S(2)}) %copy-start) | copy-done | bytes 7077912
  88.4 3.8 %collective-permute-start.6 = (f32[3,144,128]{2,1,0:T(8,128)S(1)}, f32[3,144,128]{2,1,0:T(8,128)S(1)}, u32[]{:S(2)}, u32[]{:S(2)}) collective-permute-start(f32[3,144,128]{2,1,0:T(8,128)S(1)} %get-tuple-element.47), channel_id=1, source_target_pairs={{4,8},{8,4},{12,16},{16,12},{20,24},{24,20},{5,9},{9,5},{13,17},{1... | collective-permute-start | bytes 663560 | tf_op jit(solution)/shard_map/ppermute | solution.py:686
  92.2 0.1 collective-permute-start.7
  92.3 2.6 %collective-permute-start.10 = (f32[2,288,128]{2,1,0:T(8,128)S(1)}, f32[2,288,128]{2,1,0:T(8,128)S(1)}, u32[]{:S(2)}, u32[]{:S(2)}) collective-permute-start(f32[2,288,128]{2,1,0:T(8,128)S(1)} %get-tuple-element.52), channel_id=1, source_target_pairs={{4,8},{8,4},{12,16},{16,12},{20,24},{24,20},{5,9},{9,5},{13,17},{1... | collective-permute-start | bytes 884744 | tf_op jit(solution)/shard_map/ppermute | solution.py:686
  94.9 0.1 collective-permute-start.11
  95.0 3.9 %collective-permute-done.6.rod = f32[3,144,128]{2,1,0:T(8,128)S(1)} collective-permute-done((f32[3,144,128]{2,1,0:T(8,128)S(1)}, f32[3,144,128]{2,1,0:T(8,128)S(1)}, u32[]{:S(2)}, u32[]{:S(2)}) %collective-permute-start.6) | collective-permute-done | bytes 221216 | tf_op jit(solution)/shard_map/ppermute | solution.py:686
  98.9 0.0 collective-permute-done.7.rev
  98.9 1.1 shard_map.75
  100.0 2.3 %collective-permute-start.8 = (f32[2,144,128]{2,1,0:T(8,128)S(1)}, f32[2,144,128]{2,1,0:T(8,128)S(1)}, u32[]{:S(2)}, u32[]{:S(2)}) collective-permute-start(f32[2,144,128]{2,1,0:T(8,128)S(1)} %get-tuple-element.50), channel_id=1, source_target_pairs={{4,8},{8,4},{12,16},{16,12},{20,24},{24,20},{5,9},{9,5},{13,17},{1... | collective-permute-start | bytes 442376 | tf_op jit(solution)/shard_map/ppermute | solution.py:686
  102.3 0.1 collective-permute-start.9
  102.4 2.9 %collective-permute-done.10.vod = f32[2,288,128]{2,1,0:T(8,128)S(1)} collective-permute-done((f32[2,288,128]{2,1,0:T(8,128)S(1)}, f32[2,288,128]{2,1,0:T(8,128)S(1)}, u32[]{:S(2)}, u32[]{:S(2)}) %collective-permute-start.10) | collective-permute-done | bytes 294944 | tf_op jit(solution)/shard_map/ppermute | solution.py:686
  105.2 0.0 collective-permute-done.11.vev
  105.2 2.2 %collective-permute-done.8.tod = f32[2,144,128]{2,1,0:T(8,128)S(1)} collective-permute-done((f32[2,144,128]{2,1,0:T(8,128)S(1)}, f32[2,144,128]{2,1,0:T(8,128)S(1)}, u32[]{:S(2)}, u32[]{:S(2)}) %collective-permute-start.8) | collective-permute-done | bytes 147488 | tf_op jit(solution)/shard_map/ppermute | solution.py:686
  107.4 0.0 collective-permute-done.9.tev
  107.4 3.0 %copy-done.1 = f32[6,4,2,288,128]{4,3,2,1,0:T(8,128)S(1)} copy-done((f32[6,4,2,288,128]{4,3,2,1,0:T(8,128)S(1)}, f32[6,4,2,288,128]{4,3,2,1,0:T(8,128)}, u32[]{:S(2)}) %copy-start.1) | copy-done | bytes 7077912
  110.4 17.1 %shard_map.76 = f32[8,256,256]{2,1,0:T(8,128)} custom-call(s32[8]{0:T(128)S(1)} %concatenate.9.meta, f32[2]{0:T(128)S(1)} %copy-done.4, f32[6,4,144,128]{3,2,1,0:T(8,128)S(1)} %get-tuple-element.45.gco, f32[4,144,128]{2,1,0:T(8,128)S(1)} %get-tuple-element.46.base, f32[4,144,128]{2,1,0:T(8,128)S(1)} %get-tuple-element.49.e3, ...), custom_call_target="tpu_custom_call" | custom-call | flops 1 | bytes 1 | tf_op jit(solution)/shard_map/pallas_call | solution.py:662
  (7 shorter events, 0.0 us)
Async XLA Ops:
  1.7 5.9 %copy-start.2 = (s32[8,256,256]{2,1,0:T(8,128)S(1)}, s32[8,256,256]{2,1,0:T(8,128)}, u32[]{:S(2)}) copy-start(s32[8,256,256]{2,1,0:T(8,128)} %cls.1) | copy-start | bytes 6291460
  2.7 60.5 %collective-permute-start = (f32[4,256,256]{2,1,0:T(8,128)}, f32[4,256,256]{2,1,0:T(8,128)S(1)}, u32[]{:S(2)}, u32[]{:S(2)}) collective-permute-start(f32[4,256,256]{2,1,0:T(8,128)} %pad_maximum_fusion), channel_id=1, source_target_pairs={{4,8},{8,4},{12,16},{16,12},{20,24},{24,20},{5,9},{9,5},{13,17},{1... | collective-permute-start | bytes 3145736 | tf_op jit(solution)/shard_map/ppermute | solution.py:686
  6.4 6.8 %copy-start.5 = (s32[2]{0:T(128)S(1)}, s32[2]{0:T(128)}, u32[]{:S(2)}) copy-start(s32[2]{0:T(128)} %param.11) | copy-start | bytes 28
  6.4 6.8 %copy-start.6 = (s32[2]{0:T(128)S(1)}, s32[2]{0:T(128)}, u32[]{:S(2)}) copy-start(s32[2]{0:T(128)} %param.10) | copy-start | bytes 28
  6.4 6.8 %copy-start.7 = (s32[2]{0:T(128)S(1)}, s32[2]{0:T(128)}, u32[]{:S(2)}) copy-start(s32[2]{0:T(128)} %param.12) | copy-start | bytes 28
  6.4 6.9 %copy-start.8 = (f32[8]{0:T(128)S(1)}, f32[8]{0:T(128)}, u32[]{:S(2)}) copy-start(f32[8]{0:T(128)} %param.9) | copy-start | bytes 100
  6.4 14.1 %copy-start.4 = (f32[2]{0:T(128)S(1)}, f32[2]{0:T(128)}, u32[]{:S(2)}) copy-start(f32[2]{0:T(128)} %cur.5) | copy-start | bytes 28
  7.5 55.7 %collective-permute-start.1 = (f32[4,256,256]{2,1,0:T(8,128)}, f32[4,256,256]{2,1,0:T(8,128)}, u32[]{:S(2)}, u32[]{:S(2)}) collective-permute-start(f32[4,256,256]{2,1,0:T(8,128)} %pad_maximum_fusion.1), channel_id=1, source_target_pairs={{0,4},{4,0},{8,12},{12,8},{16,20},{20,16},{24,28},{28,24},{1,5},{5... | collective-permute-start | bytes 3145736 | tf_op jit(solution)/shard_map/ppermute | solution.py:686
  9.3 9.6 %collective-permute-start.2 = (f32[2,8,16,256]{3,2,1,0:T(8,128)}, f32[2,8,16,256]{3,2,1,0:T(8,128)S(1)}, u32[]{:S(2)}, u32[]{:S(2)}) collective-permute-start(f32[2,8,16,256]{3,2,1,0:T(8,128)} %pad_maximum_fusion.2), channel_id=1, source_target_pairs={{1,2},{2,1},{5,6},{6,5},{9,10},{10,9},{13,14},{14,13},{17,18},{18,... | collective-permute-start | bytes 786440 | tf_op jit(solution)/shard_map/ppermute | solution.py:686
  13.2 7.4 %collective-permute-start.3 = (f32[2,8,16,256]{3,2,1,0:T(8,128)}, f32[2,8,16,256]{3,2,1,0:T(8,128)}, u32[]{:S(2)}, u32[]{:S(2)}) collective-permute-start(f32[2,8,16,256]{3,2,1,0:T(8,128)} %pad_maximum_fusion.3), channel_id=1, source_target_pairs={{0,1},{1,0},{2,3},{3,2},{4,5},{5,4},{6,7},{7,6},{8,9},{9,8},{10,11... | collective-permute-start | bytes 786440 | tf_op jit(solution)/shard_map/ppermute | solution.py:686
  20.6 1.6 %copy-start.3 = (f32[8,256,256]{2,1,0:T(8,128)S(1)}, f32[8,256,256]{2,1,0:T(8,128)}, u32[]{:S(2)}) copy-start(f32[8,256,256]{2,1,0:T(8,128)} %pot.1) | copy-start | bytes 6291460
  48.4 14.9 %collective-permute-start.4 = (f32[832,128]{1,0:T(8,128)S(1)}, f32[832,128]{1,0:T(8,128)S(1)}, u32[]{:S(2)}, u32[]{:S(2)}) collective-permute-start(f32[832,128]{1,0:T(8,128)S(1)} %get-tuple-element.31), channel_id=1, source_target_pairs={{4,8},{8,4},{12,16},{16,12},{20,24},{24,20},{5,9},{9,5},{13,17},{1... | collective-permute-start | bytes 1277960 | tf_op jit(solution)/shard_map/ppermute | solution.py:686
  53.1 10.2 %collective-permute-start.5 = (f32[832,128]{1,0:T(8,128)S(1)}, f32[832,128]{1,0:T(8,128)S(1)}, u32[]{:S(2)}, u32[]{:S(2)}) collective-permute-start(f32[832,128]{1,0:T(8,128)S(1)} %get-tuple-element.32), channel_id=1, source_target_pairs={{0,4},{4,0},{8,12},{12,8},{16,20},{20,16},{24,28},{28,24},{1,5},{5... | collective-permute-start | bytes 1277960 | tf_op jit(solution)/shard_map/ppermute | solution.py:686
  85.5 2.9 %copy-start = (f32[6,4,2,288,128]{4,3,2,1,0:T(8,128)}, f32[6,4,2,288,128]{4,3,2,1,0:T(8,128)S(1)}, u32[]{:S(2)}) copy-start(f32[6,4,2,288,128]{4,3,2,1,0:T(8,128)S(1)} %get-tuple-element.54.hwts) | copy-start | bytes 21233668
  88.4 10.5 %collective-permute-start.6 = (f32[3,144,128]{2,1,0:T(8,128)S(1)}, f32[3,144,128]{2,1,0:T(8,128)S(1)}, u32[]{:S(2)}, u32[]{:S(2)}) collective-permute-start(f32[3,144,128]{2,1,0:T(8,128)S(1)} %get-tuple-element.47), channel_id=1, source_target_pairs={{4,8},{8,4},{12,16},{16,12},{20,24},{24,20},{5,9},{9,5},{13,17},{1... | collective-permute-start | bytes 663560 | tf_op jit(solution)/shard_map/ppermute | solution.py:686
  92.2 6.7 %collective-permute-start.7 = (f32[3,144,128]{2,1,0:T(8,128)S(1)}, f32[3,144,128]{2,1,0:T(8,128)S(1)}, u32[]{:S(2)}, u32[]{:S(2)}) collective-permute-start(f32[3,144,128]{2,1,0:T(8,128)S(1)} %get-tuple-element.48), channel_id=1, source_target_pairs={{0,4},{4,0},{8,12},{12,8},{16,20},{20,16},{24,28},{28,24},{1,5},{5... | collective-permute-start | bytes 663560 | tf_op jit(solution)/shard_map/ppermute | solution.py:686
  92.3 12.9 %collective-permute-start.10 = (f32[2,288,128]{2,1,0:T(8,128)S(1)}, f32[2,288,128]{2,1,0:T(8,128)S(1)}, u32[]{:S(2)}, u32[]{:S(2)}) collective-permute-start(f32[2,288,128]{2,1,0:T(8,128)S(1)} %get-tuple-element.52), channel_id=1, source_target_pairs={{4,8},{8,4},{12,16},{16,12},{20,24},{24,20},{5,9},{9,5},{13,17},{1... | collective-permute-start | bytes 884744 | tf_op jit(solution)/shard_map/ppermute | solution.py:686
  94.9 10.3 %collective-permute-start.11 = (f32[2,288,128]{2,1,0:T(8,128)S(1)}, f32[2,288,128]{2,1,0:T(8,128)S(1)}, u32[]{:S(2)}, u32[]{:S(2)}) collective-permute-start(f32[2,288,128]{2,1,0:T(8,128)S(1)} %get-tuple-element.53), channel_id=1, source_target_pairs={{0,4},{4,0},{8,12},{12,8},{16,20},{20,16},{24,28},{28,24},{1,5},{5... | collective-permute-start | bytes 884744 | tf_op jit(solution)/shard_map/ppermute | solution.py:686
  100.0 7.4 %collective-permute-start.8 = (f32[2,144,128]{2,1,0:T(8,128)S(1)}, f32[2,144,128]{2,1,0:T(8,128)S(1)}, u32[]{:S(2)}, u32[]{:S(2)}) collective-permute-start(f32[2,144,128]{2,1,0:T(8,128)S(1)} %get-tuple-element.50), channel_id=1, source_target_pairs={{4,8},{8,4},{12,16},{16,12},{20,24},{24,20},{5,9},{9,5},{13,17},{1... | collective-permute-start | bytes 442376 | tf_op jit(solution)/shard_map/ppermute | solution.py:686
  102.3 5.1 %collective-permute-start.9 = (f32[2,144,128]{2,1,0:T(8,128)S(1)}, f32[2,144,128]{2,1,0:T(8,128)S(1)}, u32[]{:S(2)}, u32[]{:S(2)}) collective-permute-start(f32[2,144,128]{2,1,0:T(8,128)S(1)} %get-tuple-element.51), channel_id=1, source_target_pairs={{0,4},{4,0},{8,12},{12,8},{16,20},{20,16},{24,28},{28,24},{1,5},{5... | collective-permute-start | bytes 442376 | tf_op jit(solution)/shard_map/ppermute | solution.py:686
  107.4 3.0 %copy-start.1 = (f32[6,4,2,288,128]{4,3,2,1,0:T(8,128)S(1)}, f32[6,4,2,288,128]{4,3,2,1,0:T(8,128)}, u32[]{:S(2)}) copy-start(f32[6,4,2,288,128]{4,3,2,1,0:T(8,128)} %copy-done) | copy-start | bytes 21233668
where the time goes:
time: 128 us
  Pallas kernels  66.7 us (52%)
  waiting for transfers between devices  26.3 us (21%)
  starting transfers between devices  20.5 us (16%)
  local copies, waits for them, and re-layouts  7.57 us (6%)
  other arithmetic  6.24 us (5%)
    pallas_call x4, Pallas kernels, call(): pl.pallas_call(kernel, out_shape=[jax.ShapeDtypeStruct(shape, F32) for sh...  66.7 us
    ppermute x6, waiting for transfers between devices, swap(): lax.ppermute(od, axis, odd_pairs)  24.5 us
    ppermute x6, starting transfers between devices, swap(): lax.ppermute(od, axis, odd_pairs)  20.2 us
    unnamed x18, local copies, waits for them, and re-layouts  7.49 us
  transfers between devices with their start and end apart: 12, of which 6 were waited for; matrix products, arithmetic and copies ran while one was open for 3% of the time, Pallas kernels for 21%

commit v1 on v0

v1 whole, which is shorter than its diff:
```python
import functools

import jax
import jax.numpy as jnp
from jax import lax
from jax.experimental import pallas as pl
from jax.experimental.pallas import tpu as pltpu
from jax.sharding import PartitionSpec as P

OMEGA = 0.8
HALO = 16
PAD = 8
LANES = 128
F32 = jnp.float32
XL, XU, YL, YU, ZL, ZU = range(6)

VM = pl.BlockSpec(memory_space=pltpu.VMEM)
SM = pl.BlockSpec(memory_space=pltpu.SMEM)


class Dims:
    def __init__(self, shape):
        self.rows, self.cols, self.depth = shape
        self.halves = self.depth // LANES
        self.ext = self.cols + 2 * HALO
        self.padded = self.ext + 2 * PAD
        self.crows = self.rows // 2
        self.cext = self.ext // 2
        self.whole = [(0, self.ext)]
        side = HALO + PAD
        self.inside = [(side, self.ext - 2 * side)]
        self.strips = [(0, side), (self.ext - side, side)]


def lanes_of(rows):
    return lax.broadcasted_iota(jnp.int32, (rows, LANES), 1)


def below(parts):
    rolled = [pltpu.roll(part, 1, 1) for part in parts]
    first = lanes_of(parts[0].shape[0]) == 0
    return [rolled[0]] + [
        jnp.where(first, rolled[h - 1], rolled[h]) for h in range(1, len(parts))
    ]


def above(parts):
    rolled = [pltpu.roll(part, LANES - 1, 1) for part in parts]
    last = lanes_of(parts[0].shape[0]) == LANES - 1
    return [
        jnp.where(last, rolled[h + 1], rolled[h]) for h in range(len(parts) - 1)
    ] + [rolled[-1]]


def face(total):
    return jnp.where(total > 0, 2.0 / total, 0.0)


def lookup(cells, table):
    bits = [(cells & (1 << b)) != 0 for b in range(3)]
    level = [table[k] for k in range(8)]
    for bit in bits:
        level = [jnp.where(bit, level[k + 1], level[k]) for k in range(0, len(level), 2)]
    return level[0]


def sweep(dims, below_row, row, above_row, weights, out, scale=None, regions=None):
    for y0, size in regions or dims.whole:
        span, wide = pl.ds(y0, size), pl.ds(y0 + PAD, size)
        here = [row[h, wide, :] for h in range(dims.halves)]
        zlow, zhigh = below(here), above(here)
        for h in range(dims.halves):
            acc = weights[XL][h, span, :] * below_row[h, wide, :]
            acc += weights[XU][h, span, :] * above_row[h, wide, :]
            acc += weights[YL][h, span, :] * row[h, pl.ds(y0 + PAD - 1, size), :]
            acc += weights[YU][h, span, :] * row[h, pl.ds(y0 + PAD + 1, size), :]
            acc += weights[ZL][h, span, :] * zlow[h]
            acc += weights[ZU][h, span, :] * zhigh[h]
            if scale is None:
                out[h, wide, :] = acc + (1.0 - OMEGA) * here[h]
            else:
                out[h, span, :] = (acc - OMEGA * here[h]) * scale[h, span, :]


def sources(dims, meta, cur, count, targets, fix, regions=None):
    for s in range(count):
        row, col, dep = meta[s], meta[count + s], meta[2 * count + s]
        ext_col = col + HALO

        held = None
        for y0, size in regions or dims.whole:
            hit = (ext_col >= y0) & (ext_col < y0 + size)
            held = hit if held is None else held | hit

        @pl.when((row >= targets[0]) & (row <= targets[-1]) & held)
        def _():
            for x in targets:

                @pl.when(row == x)
                def _(x=x):
                    for h in range(dims.halves):
                        hit = lanes_of(1) == dep - h * LANES
                        fix(x, ext_col, h, jnp.where(hit, cur[s], 0.0))


def add_swept(field, scale, col, h, amount):
    field[h, pl.ds(col + PAD, 1), :] += amount / scale[h, pl.ds(col, 1), :]


def row_faces(dims, row, row_below, yl_out, zl_out, xl_out, regions=None):
    for y0, size in regions or dims.whole:
        span, wide = pl.ds(y0, size), pl.ds(y0 + PAD, size)
        here = [row[h, wide, :] for h in range(dims.halves)]
        zlow = below(here)
        zlow[0] = jnp.where(lanes_of(size) == 0, 0.0, zlow[0])
        for h in range(dims.halves):
            if xl_out is not None:
                xl_out[h, span, :] = face(here[h] + row_below[h, wide, :])
            if yl_out is not None:
                yl_out[h, wide, :] = face(here[h] + row[h, pl.ds(y0 + PAD - 1, size), :])
                zl_out[h, span, :] = face(here[h] + zlow[h])


def row_weights(dims, row, xl, xu, yl, zl, weights, scale, regions=None):
    for y0, size in regions or dims.whole:
        span, wide = pl.ds(y0, size), pl.ds(y0 + PAD, size)
        low = [zl[h, span, :] for h in range(dims.halves)]
        high = above(low)
        lane = lanes_of(size)
        top = dims.halves - 1
        high[top] = jnp.where(lane == LANES - 1, face(row[top, wide, :]), high[top])
        for h in range(dims.halves):
            parts = [
                xl[h, span, :],
                xu[h, span, :],
                yl[h, wide, :],
                yl[h, pl.ds(y0 + PAD + 1, size), :],
                low[h],
                high[h],
            ]
            diag = parts[0] + parts[1] + parts[2] + parts[3] + parts[4] + parts[5]
            gain = jnp.where(row[h, wide, :] > 0, OMEGA / diag, 0.0)
            scale[h, span, :] = diag * (1.0 / OMEGA)
            if h == 0:
                parts[ZL] = jnp.where(lane == 0, 0.0, parts[ZL])
            if h == top:
                parts[ZU] = jnp.where(lane == LANES - 1, 0.0, parts[ZU])
            for k in range(6):
                weights[k][h, span, :] = gain * parts[k]


def split_dot(field, chosen):
    total = None
    for _ in range(3):
        piece = field.astype(jnp.bfloat16)
        field = field - piece.astype(F32)
        term = jnp.dot(piece, chosen, preferred_element_type=F32)
        total = term if total is None else total + term
    return total


def picker(dims, h, lowest, highest):
    fine = lax.broadcasted_iota(jnp.int32, (LANES, LANES), 0) + h * LANES
    coarse = lax.broadcasted_iota(jnp.int32, (LANES, LANES), 1)
    hit = (fine >= 2 * coarse + lowest) & (fine <= 2 * coarse + highest)
    return jnp.where(hit, 1.0, 0.0).astype(jnp.bfloat16)


def restrict(dims, rows, offset, parities, chosen):
    total = None
    for h in range(dims.halves):
        acc = None
        for row in rows:
            for parity in parities:
                part = row[h, pl.ds(offset + parity, dims.cext, stride=2), :]
                acc = part if acc is None else acc + part
        term = split_dot(acc, chosen[h])
        total = term if total is None else total + term
    return total


def fetch_edges(parity, dim, width, pot, cls, buffers, kept, sems):
    copies = []
    for k, (pot_out, _) in enumerate(buffers):
        high = parity == (1 - k)
        start = jnp.where(high, pot.shape[dim] - width, 0)
        at = pl.ds(start, width) if dim == 0 else (slice(None), pl.ds(pl.multiple_of(start, 8), width))
        pair = [
            pltpu.make_async_copy(cls.at[at], kept.at[k], sems.at[k, 0]),
            pltpu.make_async_copy(pot.at[at], pot_out, sems.at[k, 1]),
        ]
        for copy in pair:
            copy.start()
        copies.append(pair)
    for k, (_, cls_out) in enumerate(buffers):
        copies[k][0].wait()
        cls_out[...] = kept[k].astype(F32) + 1.0
    for pair in copies:
        pair[1].wait()


def x_edge_kernel(pot, cls, od, ev, kept, sems):
    buffers = [(buf.at[pl.ds(0, 2)], buf.at[pl.ds(2, 2)]) for buf in (od, ev)]
    fetch_edges(lax.axis_index("gx") % 2, 0, 2, pot, cls, buffers, kept, sems)


def y_edge_kernel(pot, cls, od, ev, kept, sems):
    buffers = [(buf.at[0], buf.at[1]) for buf in (od, ev)]
    fetch_edges(lax.axis_index("gy") % 2, 1, HALO, pot, cls, buffers, kept, sems)


def tile_rows(dims, refs):
    rows = dims.rows
    ends, pairs = [0, rows - 1], [0, 1, rows - 2, rows - 1]
    edges = [pairs, pairs, [1, rows - 1], ends, ends]

    def getter(edge, middle, named, first):
        others = [x for x in range(first, rows) if x not in named]
        return lambda x: edge.at[named.index(x)] if x in named else middle.at[others.index(x)]

    found = [getter(refs[k], refs[5 + k], edges[k], int(k == 2)) for k in range(5)]
    return found + list(refs[10:13])


def own_rows(dims, nsrc, meta, cur, res, vol, fx, fy, fz, wts, scl, one, regions, face_regions):
    rows = dims.rows
    for x in range(rows):
        row_faces(
            dims,
            res(x),
            res(x - 1) if x else None,
            fy(x),
            fz(x),
            fx(x) if x else None,
            face_regions,
        )
    weights = lambda x: [wts.at[k, x - 1] for k in range(6)]
    for x in range(1, rows - 1):
        row_weights(
            dims, res(x), fx(x), fx(x + 1), fy(x), fz(x), weights(x),
            scl.at[x - 1], regions,
        )
    for x in range(1, rows - 1):
        sweep(
            dims, vol(x - 1), vol(x), vol(x + 1), weights(x), one.at[x - 1],
            regions=regions,
        )
    sources(
        dims, meta, cur, nsrc, range(1, rows - 1),
        lambda x, *rest: add_swept(one.at[x - 1], scl.at[x - 1], *rest),
        regions,
    )


def tile_kernel(dims, nsrc, meta, cur, table, pot, cls, *refs):
    res, vol, fx, fy, fz, wts, scl, one = tile_rows(dims, refs)
    margin = PAD + HALO
    for x in range(dims.rows):
        for h in range(dims.halves):
            lanes = slice(h * LANES, (h + 1) * LANES)
            zero = jnp.zeros((margin, LANES), F32)
            for ref in (res, vol):
                ref(x)[h, pl.ds(0, margin), :] = zero
                ref(x)[h, pl.ds(margin + dims.cols, margin), :] = zero
            vol(x)[h, pl.ds(margin, dims.cols), :] = pot[x, :, lanes]
            res(x)[h, pl.ds(margin, dims.cols), :] = lookup(cls[x, :, lanes], table)
    own_rows(dims, nsrc, meta, cur, res, vol, fx, fy, fz, wts, scl, one, dims.inside,
             [(HALO, dims.cols)])


def strip_kernel(dims, nsrc, meta, cur, table, yod, yev, *refs):
    count = len(dims.tile)
    res_edge, vol_edge = refs[count], refs[count + 1]
    res, vol, fx, fy, fz, wts, scl, one = tile_rows(dims, refs[count : 2 * count])
    send_od, send_ev = refs[2 * count :]
    rows, halves, cols = dims.rows, dims.halves, dims.cols
    odd_x, odd_y = meta[3 * nsrc] == 1, meta[3 * nsrc + 1] == 1
    for x in range(rows):
        for h in range(halves):
            lanes = slice(h * LANES, (h + 1) * LANES)
            for into, take_ev in ((PAD, True), (PAD + HALO + cols, False)):
                pair = []
                for k in range(2):
                    a, b = yod[k, x, :, lanes], yev[k, x, :, lanes]
                    pair.append(jnp.where(odd_y, b, a) if take_ev else jnp.where(odd_y, a, b))
                vol(x)[h, pl.ds(into, HALO), :] = pair[0]
                number = pair[1].astype(jnp.int32)
                res(x)[h, pl.ds(into, HALO), :] = jnp.where(
                    number > 0, lookup(number - 1, table), 0.0
                )
            fy(x)[h, pl.ds(PAD + dims.ext, PAD), :] = jnp.zeros((PAD, LANES), F32)
    own_rows(dims, nsrc, meta, cur, res, vol, fx, fy, fz, wts, scl, one, dims.strips, dims.strips)

    def fill(send, high):
        edge = jnp.where(high, 2, 0)
        inner = jnp.where(high, rows - 2, 1)
        for h in range(halves):
            send[pl.ds(h * dims.ext, dims.ext), :] = one[inner - 1, h, pl.ds(PAD, dims.ext), :]
        base = halves * dims.ext
        for k in range(4):
            ref = vol_edge if k < 2 else res_edge
            for h in range(halves):
                at = base + (k * halves + h) * 2 * HALO
                send[pl.ds(at, HALO), :] = ref[edge + k % 2, h, pl.ds(PAD, HALO), :]
                send[pl.ds(at + HALO, HALO), :] = ref[
                    edge + k % 2, h, pl.ds(PAD + HALO + cols, HALO), :
                ]

    fill(send_od, odd_x)
    fill(send_ev, jnp.logical_not(odd_x))


def first_kernel(dims, nsrc, meta, cur, *refs):
    res, vol, fx, fy, fz, wts, scl, one = tile_rows(dims, refs[: len(dims.tile)])
    two, rsd, cfc, gco, ins = refs[len(dims.tile) + 1 :]
    rows, halves = dims.rows, dims.halves
    weights = lambda x: [wts.at[k, x - 1] for k in range(6)]
    for x in range(2, rows - 2):
        sweep(dims, one.at[x - 2], one.at[x - 1], one.at[x], weights(x), two.at[x - 2])

    sources(
        dims, meta, cur, nsrc, range(2, rows - 2),
        lambda x, *rest: add_swept(two.at[x - 2], scl.at[x - 1], *rest),
    )

    for x in range(3, rows - 3):
        sweep(
            dims, two.at[x - 3], two.at[x - 2], two.at[x - 1], weights(x), rsd.at[x - 3],
            scl.at[x - 1],
        )

    def fix_rsd(row, col, h, amount):
        rsd[row - 3, h, pl.ds(col, 1), :] += amount

    sources(dims, meta, cur, nsrc, range(3, rows - 3), fix_rsd)

    both = [picker(dims, h, 0, 1) for h in range(halves)]
    even = [picker(dims, h, 0, 0) for h in range(halves)]
    n = dims.crows
    for c in range(n):
        pair = lambda row: [row(2 * c), row(2 * c + 1)]
        if c:
            cfc[c] = restrict(dims, [fx(2 * c)], 0, (0, 1), both)
        cfc[n + 1 + c] = restrict(dims, pair(fy), PAD, (0,), both)
        cfc[2 * n + 1 + c] = restrict(dims, pair(fz), 0, (0, 1), even)
        top = None
        for row in pair(res):
            for parity in (0, 1):
                part = face(row[halves - 1, pl.ds(PAD + parity, dims.cext, stride=2), :])
                top = part if top is None else top + part
        cfc[3 * n + 1 + c] = top
        ins[c] = res(2 * c)[0, pl.ds(PAD, dims.cext, stride=2), :]
    for c in range(1, n - 1):
        for k, part in enumerate(coarse_weights(dims, cfc, ins, c, cfc[c], cfc[c + 1])):
            gco[k, c - 1] = part


def coarse_weights(dims, cfc, ins, c, xl, xu):
    n = dims.crows
    lane = lanes_of(dims.cext)
    yl, zl = cfc[n + 1 + c], cfc[2 * n + 1 + c]
    yu = pltpu.roll(yl, dims.cext - 1, 0)
    zu = jnp.where(lane == LANES - 1, cfc[3 * n + 1 + c], pltpu.roll(zl, LANES - 1, 1))
    diag = xl + xu + yl + yu + zl + zu
    gain = jnp.where(ins[c] > 0, OMEGA / diag, 0.0)
    zl = jnp.where(lane == 0, 0.0, zl)
    zu = jnp.where(lane == LANES - 1, 0.0, zu)
    return [gain * part for part in (xl, xu, yl, yu, zl, zu)] + [gain]


def neighbours(rows):
    ext = rows.shape[0]
    return (
        pltpu.roll(rows, 1, 0),
        pltpu.roll(rows, ext - 1, 0),
        pltpu.roll(rows, 1, 1),
        pltpu.roll(rows, LANES - 1, 1),
    )


def coarse_side(field, base, weights):
    ylow, yhigh, zlow, zhigh = neighbours(field)
    return (
        (1.0 - OMEGA) * field
        + base
        + weights[YL] * ylow
        + weights[YU] * yhigh
        + weights[ZL] * zlow
        + weights[ZU] * zhigh
    )


def edge_sweep(dims, nsrc, meta, cur, res, vol, fx, fy, fz, hres, hvol, hfx, hfy, hfz, hwts, hscl,
               edge, regions, face_regions):
    rows = dims.rows
    last = rows - 1
    row_faces(dims, hres.at[1], hres.at[0], hfy.at[0], hfz.at[0], hfx.at[0], face_regions)
    row_faces(dims, res.at[0], hres.at[1], None, None, hfx.at[1], face_regions)
    row_faces(dims, hres.at[2], res.at[3], hfy.at[1], hfz.at[1], hfx.at[2], face_regions)
    row_faces(dims, hres.at[3], hres.at[2], None, None, hfx.at[3], face_regions)
    weights = lambda k: [hwts.at[j, k] for j in range(6)]
    for k, (row, xl, xu, yl, zl) in enumerate((
        (hres.at[1], hfx.at[0], hfx.at[1], hfy.at[0], hfz.at[0]),
        (res.at[0], hfx.at[1], fx.at[0], fy.at[0], fz.at[0]),
        (res.at[3], fx.at[1], hfx.at[2], fy.at[1], fz.at[1]),
        (hres.at[2], hfx.at[2], hfx.at[3], hfy.at[1], hfz.at[1]),
    )):
        row_weights(dims, row, xl, xu, yl, zl, weights(k), hscl.at[k], regions)
    for k, line in enumerate((
        (hvol.at[0], hvol.at[1], vol.at[0]),
        (hvol.at[1], vol.at[0], vol.at[1]),
        (vol.at[2], vol.at[3], hvol.at[2]),
        (vol.at[3], hvol.at[2], hvol.at[3]),
    )):
        sweep(dims, *line, weights(k), edge.at[k + 1], regions=regions)
    index = {-1: 0, 0: 1, last: 2, rows: 3}
    sources(
        dims, meta, cur, nsrc, (-1, 0, last, rows),
        lambda x, *rest: add_swept(edge.at[index[x] + 1], hscl.at[index[x]], *rest),
        regions,
    )


def edge_kernel(dims, nsrc, meta, cur, table, xod, xev, res, vol, fx, fy, fz, hres, hvol, hfx, hfy,
                hfz, hwts, hscl, edge):
    halves, cols = dims.halves, dims.cols
    odd_x = meta[3 * nsrc] == 1
    margin = PAD + HALO
    for side in range(2):
        choose = lambda a, b: jnp.where(odd_x, b, a) if side == 0 else jnp.where(odd_x, a, b)
        for k in range(2):
            for h in range(halves):
                lanes = slice(h * LANES, (h + 1) * LANES)
                zero = jnp.zeros((margin, LANES), F32)
                for ref in (hres, hvol):
                    ref[2 * side + k, h, pl.ds(0, margin), :] = zero
                    ref[2 * side + k, h, pl.ds(margin + cols, margin), :] = zero
                wide = pl.ds(margin, cols)
                hvol[2 * side + k, h, wide, :] = choose(xod[k, :, lanes], xev[k, :, lanes])
                number = choose(xod[2 + k, :, lanes], xev[2 + k, :, lanes]).astype(jnp.int32)
                hres[2 * side + k, h, wide, :] = jnp.where(
                    number > 0, lookup(number - 1, table), 0.0
                )
        for h in range(halves):
            hfy[side, h, pl.ds(PAD + dims.ext, PAD), :] = jnp.zeros((PAD, LANES), F32)
    edge_sweep(dims, nsrc, meta, cur, res, vol, fx, fy, fz, hres, hvol, hfx, hfy, hfz, hwts, hscl,
               edge, dims.inside, [(HALO, cols)])


def second_kernel(dims, nsrc, meta, cur, sod, sev, wts, scl, one, two, rsd, res, vol, fx, fy, fz,
                  cfc, gci, ins, *refs):
    rows, halves, cols = dims.rows, dims.halves, dims.cols
    hres, hvol, hfx, hfy, hfz, hwts, hscl, edge, htwo, gco, base, c_od, c_ev, v_od, v_ev, redge = (
        refs[8:]
    )
    odd_x = meta[3 * nsrc] == 1
    last = rows - 1
    for side in range(2):
        choose = lambda a, b: jnp.where(odd_x, b, a) if side == 0 else jnp.where(odd_x, a, b)
        for h in range(halves):
            for k in range(2):
                for ref, kind in ((hvol, k), (hres, 2 + k)):
                    strip = halves * dims.ext + (kind * halves + h) * 2 * HALO
                    low = pl.ds(strip, HALO)
                    high = pl.ds(strip + HALO, HALO)
                    ref[2 * side + k, h, pl.ds(PAD, HALO), :] = choose(sod[low, :], sev[low, :])
                    ref[2 * side + k, h, pl.ds(PAD + HALO + cols, HALO), :] = choose(
                        sod[high, :], sev[high, :]
                    )
            span = pl.ds(h * dims.ext, dims.ext)
            edge[5 * side, h, pl.ds(PAD, dims.ext), :] = choose(sod[span, :], sev[span, :])
    edge_sweep(dims, nsrc, meta, cur, res, vol, fx, fy, fz, hres, hvol, hfx, hfy, hfz, hwts, hscl,
               edge, dims.strips, dims.strips)

    outer = lambda x: x + 1 if x <= 0 else x - last + 2
    inner = lambda x: 1 <= x <= last - 1
    weights = lambda x: [
        wts.at[k, x - 1] if inner(x) else hwts.at[k, outer(x)] for k in range(6)
    ]
    scale = lambda x: scl.at[x - 1] if inner(x) else hscl.at[outer(x)]

    def swept(x):
        if x <= 0:
            return edge.at[x + 2]
        return one.at[x - 1] if x < last else edge.at[x - last + 3]

    def twice(x):
        if x <= 1:
            return htwo.at[x + 1]
        return two.at[x - 2] if x < last - 1 else htwo.at[x - last + 4]

    for x in (-1, 0, 1, last - 1, last, rows):
        sweep(dims, swept(x - 1), swept(x), swept(x + 1), weights(x), twice(x))
    sources(
        dims, meta, cur, nsrc, (-1, 0, 1, last - 1, last, rows),
        lambda x, *rest: add_swept(twice(x), scale(x), *rest),
    )
    pick_od = jnp.where(odd_x, 3, 2)
    pick_ev = jnp.where(odd_x, 2, 3)
    for h in range(halves):
        v_od[h, :, :] = htwo[pick_od, h, pl.ds(PAD, dims.ext), :]
        v_ev[h, :, :] = htwo[pick_ev, h, pl.ds(PAD, dims.ext), :]

    def resid_row(x):
        if x <= 2:
            return redge.at[x]
        return rsd.at[x - 3] if x < last - 2 else redge.at[x - last + 5]

    for x in (0, 1, 2, last - 2, last - 1, last):
        sweep(
            dims, twice(x - 1), twice(x), twice(x + 1), weights(x), resid_row(x), scale(x)
        )

    def fix_rsd(x, col, h, amount):
        resid_row(x)[h, pl.ds(col, 1), :] += amount

    sources(dims, meta, cur, nsrc, (0, 1, 2, last - 2, last - 1, last), fix_rsd)

    both = [picker(dims, h, 0, 1) for h in range(halves)]
    n = dims.crows
    bottom = restrict(dims, [hfx.at[1]], 0, (0, 1), both)
    topmost = restrict(dims, [hfx.at[2]], 0, (0, 1), both)

    e1, gc = [], []
    for c in range(n):
        total = restrict(dims, [resid_row(2 * c), resid_row(2 * c + 1)], 0, (0, 1), both)
        if 0 < c < n - 1:
            parts = [gci[k, c - 1] for k in range(7)]
        else:
            xl = bottom if c == 0 else cfc[c]
            xu = topmost if c == n - 1 else cfc[c + 1]
            parts = coarse_weights(dims, cfc, ins, c, xl, xu)
            for k in range(6):
                gco[k, 0 if c == 0 else 1] = parts[k]
        gc.append(parts)
        e1.append(parts[6] * total)
        base[c] = e1[c]

    low = (e1[0], coarse_side(e1[0], e1[0], gc[0]) + gc[0][XU] * e1[1], gc[0][XL])
    high = (
        e1[n - 1],
        coarse_side(e1[n - 1], e1[n - 1], gc[n - 1]) + gc[n - 1][XL] * e1[n - 2],
        gc[n - 1][XU],
    )
    for k in range(3):
        c_od[k] = jnp.where(odd_x, high[k], low[k])
        c_ev[k] = jnp.where(odd_x, low[k], high[k])


def coarse_row(dims, gci, gco, c):
    if 0 < c < dims.crows - 1:
        return [gci[k, c - 1] for k in range(6)]
    return [gco[k, 0 if c == 0 else 1] for k in range(6)]


def third_kernel(dims, nsrc, meta, gci, gco, base, rod, rev, e3, c_od, c_ev):
    n = dims.crows
    odd_x = meta[3 * nsrc] == 1
    low = [jnp.where(odd_x, rev[k], rod[k]) for k in range(3)]
    high = [jnp.where(odd_x, rod[k], rev[k]) for k in range(3)]
    gc = lambda c: coarse_row(dims, gci, gco, c)

    def coarse_sweep(field, under, over):
        out = []
        for c in range(n):
            w = gc(c)
            new = coarse_side(field[c], base[c], w)
            new += w[XL] * (field[c - 1] if c else under)
            new += w[XU] * (field[c + 1] if c < n - 1 else over)
            out.append(new)
        return out

    e1 = [base[c] for c in range(n)]
    e2 = coarse_sweep(e1, low[0], high[0])
    under = low[1] + low[2] * e1[0]
    over = high[1] + high[2] * e1[n - 1]
    out = coarse_sweep(e2, under, over)
    for c in range(n):
        e3[c] = out[c]
    w = gc(0)
    first = (out[0], coarse_side(out[0], base[0], w) + w[XU] * out[1])
    w = gc(n - 1)
    final = (out[n - 1], coarse_side(out[n - 1], base[n - 1], w) + w[XL] * out[n - 2])
    for k in range(2):
        c_od[k] = jnp.where(odd_x, final[k], first[k])
        c_ev[k] = jnp.where(odd_x, first[k], final[k])


def fourth_kernel(dims, nsrc, meta, cur, gci, gco, base, e3, rod, rev, tod, tev, vod, vev, wts, scl,
                  two, hwts, hscl, htwo, out, raised, zero, three, done, sems):
    rows, halves, cols = dims.rows, dims.halves, dims.cols
    n = dims.crows
    odd_x = meta[3 * nsrc] == 1
    below_of = lambda od, ev: jnp.where(odd_x, ev, od)
    above_of = lambda od, ev: jnp.where(odd_x, od, ev)
    field = [e3[c] for c in range(n)]
    under = below_of(tod[1], tev[1]) + below_of(rod[2], rev[2]) * field[0]
    over = above_of(tod[1], tev[1]) + above_of(rod[2], rev[2]) * field[n - 1]
    e4 = [under]
    for c in range(n):
        w = coarse_row(dims, gci, gco, c)
        new = coarse_side(field[c], base[c], w)
        new += w[XL] * (field[c - 1] if c else below_of(tod[0], tev[0]))
        new += w[XU] * (field[c + 1] if c < n - 1 else above_of(tod[0], tev[0]))
        e4.append(new)
    e4.append(over)
    spread = []
    for h in range(halves):
        fine = lax.broadcasted_iota(jnp.int32, (LANES, LANES), 1) + h * LANES
        coarse = lax.broadcasted_iota(jnp.int32, (LANES, LANES), 0)
        hit = (fine >= 2 * coarse) & (fine <= 2 * coarse + 1)
        spread.append(jnp.where(hit, 1.0, 0.0).astype(jnp.bfloat16))
    for c in range(n + 2):
        for h in range(halves):
            lifted = split_dot(e4[c], spread[h])
            raised[c, h, pl.ds(0, dims.cext, stride=2), :] = lifted
            raised[c, h, pl.ds(1, dims.cext, stride=2), :] = lifted

    last = rows - 1

    def twice(x):
        if x <= 1:
            return htwo.at[x + 1]
        return two.at[x - 2] if x < last - 1 else htwo.at[x - last + 4]

    outer = lambda x: x + 1 if x <= 0 else x - last + 2
    inner = lambda x: 1 <= x <= last - 1
    weights = lambda x: [
        wts.at[k, x - 1] if inner(x) else hwts.at[k, outer(x)] for k in range(6)
    ]
    scale = lambda x: scl.at[x - 1] if inner(x) else hscl.at[outer(x)]
    for x in range(-2, rows + 2):
        for h in range(halves):
            wide = pl.ds(PAD, dims.ext)
            if x == -2:
                value = below_of(vod[h, :, :], vev[h, :, :])
            elif x == rows + 1:
                value = above_of(vod[h, :, :], vev[h, :, :])
            else:
                value = twice(x)[h, wide, :]
            zero[x + 2, h, wide, :] = value + raised[(x + 2) // 2, h, :, :]
    for x in range(-1, rows + 1):
        sweep(dims, zero.at[x + 1], zero.at[x + 2], zero.at[x + 3], weights(x), three.at[x + 1])
    sources(
        dims, meta, cur, nsrc, range(-1, rows + 1),
        lambda x, *rest: add_swept(three.at[x + 1], scale(x), *rest),
    )
    copies = []
    for x in range(rows):
        last_sweep(
            dims, nsrc, meta, cur, x, three.at[x], three.at[x + 1], three.at[x + 2], weights(x),
            scale(x), done.at[x],
        )
        copy = pltpu.make_async_copy(done.at[x], out.at[x], sems.at[x])
        copy.start()
        copies.append(copy)
    for copy in copies:
        copy.wait()


def last_sweep(dims, nsrc, meta, cur, x, below_row, row, above_row, w, scale, done):
    halves = dims.halves

    at, size = PAD + HALO, dims.cols
    here = [row[h, pl.ds(at, size), :] for h in range(halves)]
    zlow, zhigh = below(here), above(here)
    for h in range(halves):
        span = pl.ds(HALO, size)
        acc = w[XL][h, span, :] * below_row[h, pl.ds(at, size), :]
        acc += w[XU][h, span, :] * above_row[h, pl.ds(at, size), :]
        acc += w[YL][h, span, :] * row[h, pl.ds(at - 1, size), :]
        acc += w[YU][h, span, :] * row[h, pl.ds(at + 1, size), :]
        acc += w[ZL][h, span, :] * zlow[h]
        acc += w[ZU][h, span, :] * zhigh[h]
        done[:, h * LANES : (h + 1) * LANES] = acc + (1.0 - OMEGA) * here[h]
    for s in range(nsrc):
        r, col, dep = meta[s], meta[nsrc + s], meta[2 * nsrc + s]

        @pl.when((r == x) & (col >= 0) & (col < dims.cols))
        def _():
            for h in range(halves):
                block = pl.multiple_of(col // 8 * 8, 8)
                place = lax.broadcasted_iota(jnp.int32, (8, LANES), 0) + block
                hit = (lanes_of(8) == dep - h * LANES) & (place == col)
                amount = jnp.where(hit, cur[s], 0.0)
                done[pl.ds(block, 8), h * LANES : (h + 1) * LANES] += (
                    amount / scale[h, pl.ds(block + HALO, 8), :]
                )


def call(kernel, outs, ins, specs, scratch=(), aliases=None, out_specs=None, limit=24, cost=1):
    return pl.pallas_call(
        kernel,
        out_shape=[jax.ShapeDtypeStruct(shape, F32) for shape in outs],
        in_specs=specs,
        out_specs=out_specs if out_specs is not None else [VM] * len(outs),
        scratch_shapes=list(scratch),
        input_output_aliases=aliases or {},
        compiler_params=pltpu.CompilerParams(vmem_limit_bytes=limit * 2**20),
        cost_estimate=pl.CostEstimate(flops=cost, bytes_accessed=cost, transcendentals=0),
    )(*ins)


def swaps(count):
    pairs = []
    for first in (1, 0):
        found = []
        for low in range(first, count - 1, 2):
            found += [(low, low + 1), (low + 1, low)]
        pairs.append(found)
    return pairs


def swap(od, ev, axis):
    odd_pairs, even_pairs = swaps(lax.axis_size(axis))
    return lax.ppermute(od, axis, odd_pairs), lax.ppermute(ev, axis, even_pairs)


def per_device(potential, classes, sigma_table, row_index, col_index, depth_index, currents):
    dims = Dims(potential.shape)
    rows, cols, depth = potential.shape
    halves, ext, padded, n, cext = dims.halves, dims.ext, dims.padded, dims.crows, dims.cext
    nsrc = row_index.shape[0]
    gx, gy = lax.axis_index("gx"), lax.axis_index("gy")
    odd_x, odd_y = gx % 2, gy % 2
    meta = jnp.concatenate(
        [
            row_index - gx * rows,
            col_index - gy * cols,
            depth_index,
            jnp.stack([odd_x, odd_y]),
        ]
    ).astype(jnp.int32)
    table = 1.0 / sigma_table

    bind = lambda kernel: functools.partial(kernel, dims, nsrc)
    wide = lambda k: (k, halves, padded, LANES)
    flat = lambda k: (k, halves, ext, LANES)
    send = (halves * ext + 4 * halves * 2 * HALO, LANES)
    coarse = lambda *k: (*k, cext, LANES)
    vmem = lambda *shapes: [pltpu.VMEM(shape, F32) for shape in shapes]
    hbm = pl.BlockSpec(memory_space=pl.ANY)
    far = pl.BlockSpec(memory_space=pltpu.HBM)

    def edges(kernel, shape, kept):
        return call(
            kernel, [shape] * 2, [potential, classes], [far] * 2,
            scratch=[pltpu.VMEM((2, *kept), jnp.int32), pltpu.SemaphoreType.DMA((2, 2))],
            limit=54,
        )

    xod, xev = swap(*edges(x_edge_kernel, (4, cols, depth), (2, cols, depth)), "gx")
    yod, yev = swap(
        *edges(y_edge_kernel, (2, rows, HALO, depth), (rows, HALO, depth)), "gy"
    )
    tile = dims.tile = [
        wide(4), wide(4), flat(2), wide(2), flat(2), wide(rows - 4), wide(rows - 4),
        flat(rows - 3), wide(rows - 2), flat(rows - 2), (6, *flat(rows - 2)), flat(rows - 2),
        wide(rows - 2),
    ]
    parts = call(
        bind(tile_kernel), tile, [meta, currents, table, potential, classes],
        [SM] * 3 + [VM] * 2,
        limit=4,
    )
    parts = call(
        bind(strip_kernel),
        tile + [send, send],
        [meta, currents, table, yod, yev, *parts],
        [SM] * 3 + [VM] * (2 + len(tile)),
        aliases={5 + k: k for k in range(len(tile))},
        limit=4,
    )
    res, vol, fx, fy, fz = parts[:5]
    wts, scl, one, s_od, s_ev = parts[10:]
    sod, sev = swap(s_od, s_ev, "gx")
    (two, rsd, cfc, gci, ins) = call(
        bind(first_kernel),
        [wide(rows - 4), flat(rows - 6), coarse(4 * n + 1), coarse(7, n - 2), coarse(n)],
        [meta, currents, *parts[: len(tile) + 1]],
        [SM] * 2 + [VM] * (len(tile) + 1),
        limit=4,
    )
    held = [wide(4), wide(4), flat(4), wide(2), flat(2), (6, *flat(4)), flat(4), wide(6)]
    edges = call(
        bind(edge_kernel),
        held,
        [meta, currents, table, xod, xev, res, vol, fx, fy, fz],
        [SM] * 3 + [VM] * 7,
        limit=4,
    )
    ins_of = [meta, currents, sod, sev, wts, scl, one, two, rsd, res, vol, fx, fy, fz, cfc, gci, ins]
    outs = call(
        bind(second_kernel),
        held + [wide(6), coarse(6, 2), coarse(n), coarse(3), coarse(3)] + [flat(1)[1:]] * 2,
        ins_of + list(edges),
        [SM] * 2 + [VM] * (len(ins_of) - 2 + len(held)),
        scratch=vmem(flat(6)),
        aliases={len(ins_of) + k: k for k in range(len(held))},
        limit=4,
    )
    hwts, hscl, (htwo, gco, base, c_od, c_ev, v_od, v_ev) = outs[5], outs[6], outs[8:]
    rod, rev = swap(c_od, c_ev, "gx")
    vod, vev = swap(v_od, v_ev, "gx")
    (e3, t_od, t_ev) = call(
        bind(third_kernel),
        [coarse(n), coarse(2), coarse(2)],
        [meta, gci, gco, base, rod, rev],
        [SM] + [VM] * 5,
        limit=4,
    )
    tod, tev = swap(t_od, t_ev, "gx")
    (out,) = call(
        bind(fourth_kernel),
        [(rows, cols, depth)],
        [meta, currents, gci, gco, base, e3, rod, rev, tod, tev, vod, vev, wts, scl, two, hwts,
         hscl, htwo],
        [SM] * 2 + [VM] * 16,
        scratch=vmem(flat(n + 2), wide(rows + 4), wide(rows + 2), (rows, cols, depth))
        + [pltpu.SemaphoreType.DMA((rows,))],
        out_specs=[hbm],
        limit=13,
    )
    return out


def solution(mesh):
    tiled = P("gx", "gy", None)
    return jax.shard_map(
        per_device,
        mesh=mesh,
        in_specs=(tiled, tiled, P(), P(), P(), P(), P()),
        out_specs=tiled,
        check_vma=False,
    )
```

time: 128 us -> 72.5 us (0.57)
  Pallas kernels: 66.7 us -> 34.2 us
  waiting for transfers between devices: 26.3 us -> 13.1 us
  other arithmetic: 6.24 us -> 0.01 us
  local copies, waits for them, and re-layouts: 7.57 us -> 3.9 us
    pallas_call x4 -> x9, Pallas kernels: 66.7 us -> 34.2 us  [call(): pl.pallas_call(kernel, out_shape=[jax.ShapeDtypeStruct(shape, F32) for sh...]
    ppermute x6, waiting for transfers between devices: 24.5 us -> 12.8 us  [swap(): lax.ppermute(od, axis, odd_pairs)]
    unnamed x18, local copies, waits for them, and re-layouts: 7.49 us -> 3.82 us
    another operation x3 -> x0, other arithmetic: 2.45 us -> none  [the longest x2 1.72 us: per_device(): jnp.stack(edges(1, HALO, odd_y == 0))]
    concatenate x2 -> x0, other arithmetic: 2.13 us -> none  [the longest x1 1.09 us: per_device(): jnp.concatenate(edges(0, 2, odd_x == 0))]
    ppermute x6, starting transfers between devices: 20.2 us -> 18.5 us  [swap(): lax.ppermute(od, axis, odd_pairs)]
    add x1 -> x0, other arithmetic: 1.66 us -> none  [edges(): lax.dynamic_slice_in_dim(classes, start, width, dim).astype(F32) + 1.0]
    ppermute x6, starting transfers between devices: 0.29 us -> 1.92 us  [swap(): lax.ppermute(ev, axis, even_pairs)]
  transfers between devices with their start and end apart: 12 -> 12, of which waited for: 6 -> 6; matrix products, arithmetic and copies ran while one was open for 3% -> 0% of each run, Pallas kernels for 21% -> 26%
where the time goes in v1:
time: 72.5 us; the launch traced here: 72.1 us
  Pallas kernels  34.2 us (47%)
  starting transfers between devices  20.4 us (28%)
  waiting for transfers between devices  13.1 us (18%)
  local copies, waits for them, and re-layouts  3.9 us (5%)
    pallas_call x9, Pallas kernels, call(): pl.pallas_call(kernel, out_shape=[jax.ShapeDtypeStruct(shape, F32) for sh...  34.2 us
    ppermute x6, starting transfers between devices, swap(): lax.ppermute(od, axis, odd_pairs)  18.5 us
    ppermute x6, waiting for transfers between devices, swap(): lax.ppermute(od, axis, odd_pairs)  12.8 us
    unnamed x18, local copies, waits for them, and re-layouts  3.82 us
    ppermute x6, starting transfers between devices, swap(): lax.ppermute(ev, axis, even_pairs)  1.92 us
  transfers between devices with their start and end apart: 12, of which 6 were waited for; matrix products, arithmetic and copies ran while one was open for 0% of the time, Pallas kernels for 26%

profile of v1, /device:TPU:11, one launch (start us, length us, event | category | flops | bytes accessed | tf_op | source)
XLA Modules:
  0.0 72.1 jit_solution(5413855811976610784)
XLA Ops:
  0.0 2.9 %shard_map.77 = (f32[4,256,256]{2,1,0:T(8,128)}, f32[4,256,256]{2,1,0:T(8,128)}) custom-call(f32[8,256,256]{2,1,0:T(8,128)} %pot.5, s32[8,256,256]{2,1,0:T(8,128)} %cls.5), custom_call_target="tpu_custom_call" | custom-call | flops 1 | bytes 1 | tf_op jit(solution)/shard_map/pallas_call | solution.py:692
  2.9 3.7 %collective-permute-start.4 = (f32[4,256,256]{2,1,0:T(8,128)}, f32[4,256,256]{2,1,0:T(8,128)S(1)}, u32[]{:S(2)}, u32[]{:S(2)}) collective-permute-start(f32[4,256,256]{2,1,0:T(8,128)} %get-tuple-element.97), channel_id=1, source_target_pairs={{4,8},{8,4},{12,16},{16,12},{20,24},{24,20},{5,9},{9,5},{13,17},{1... | collective-permute-start | bytes 3145736 | tf_op jit(solution)/shard_map/ppermute | solution.py:716
  6.6 0.0 copy-start.5
  6.6 0.0 copy-start.6
  6.6 0.0 copy-start.7
  6.6 0.0 copy-start.8
  6.6 0.0 copy-start
  6.6 0.0 copy-start.4
  6.7 0.1 collective-permute-start.5
  6.7 2.1 %shard_map.73 = (f32[2,8,16,256]{3,2,1,0:T(8,128)}, f32[2,8,16,256]{3,2,1,0:T(8,128)}) custom-call(f32[8,256,256]{2,1,0:T(8,128)} %pot.5, s32[8,256,256]{2,1,0:T(8,128)} %cls.5), custom_call_target="tpu_custom_call" | custom-call | flops 1 | bytes 1 | tf_op jit(solution)/shard_map/pallas_call | solution.py:692
  8.8 3.2 %collective-permute-start = (f32[2,8,16,256]{3,2,1,0:T(8,128)}, f32[2,8,16,256]{3,2,1,0:T(8,128)S(1)}, u32[]{:S(2)}, u32[]{:S(2)}) collective-permute-start(f32[2,8,16,256]{3,2,1,0:T(8,128)} %get-tuple-element.62), channel_id=1, source_target_pairs={{1,2},{2,1},{5,6},{6,5},{9,10},{10,9},{13,14},{14,13},{17,18},{18,... | collective-permute-start | bytes 786440 | tf_op jit(solution)/shard_map/ppermute | solution.py:716
  12.0 0.1 collective-permute-start.1
  12.1 0.0 copy-done.5
  12.1 0.0 copy-done.6
  12.2 0.0 copy-done.7
  12.2 0.1 concatenate.3.meta
  12.3 0.0 copy-done
  12.3 0.0 copy-start.1
  12.3 1.6 %copy-done.1 = s32[8,256,256]{2,1,0:T(8,128)S(1)} copy-done((s32[8,256,256]{2,1,0:T(8,128)S(1)}, s32[8,256,256]{2,1,0:T(8,128)}, u32[]{:S(2)}) %copy-start.1) | copy-done | bytes 2097176
  13.9 5.5 %shard_map.74 = (f32[4,2,304,128]{3,2,1,0:T(8,128)S(1)}, f32[4,2,304,128]{3,2,1,0:T(8,128)S(1)}, f32[2,2,288,128]{3,2,1,0:T(8,128)S(1)}, f32[2,2,304,128]{3,2,1,...) custom-call(s32[8]{0:T(128)S(1)} %concatenate.3.meta, ...), custom_call_target="tpu_custom_call" | custom-call | flops 1 | bytes 1 | tf_op jit(solution)/shard_map/pallas_call | solution.py:692
  19.4 0.0 collective-permute-done.yod
  19.4 0.3 collective-permute-done.1.yev
  19.6 1.9 %shard_map.75 = (f32[4,2,304,128]{3,2,1,0:T(8,128)S(1)}, f32[4,2,304,128]{3,2,1,0:T(8,128)S(1)}, f32[2,2,288,128]{3,2,1,0:T(8,128)S(1)}, f32[2,2,304,128]{3,2,1,...) custom-call(s32[8]{0:T(128)S(1)} %concatenate.3.meta, ...), custom_call_target="tpu_custom_call", output_to_operand_aliasing={{0}: (5, {}), {1}: (6, {}), {2}: (7, {}), {3}: (8, {}), {4}... | custom-call | flops 1 | bytes 1 | tf_op jit(solution)/shard_map/pallas_call | solution.py:692
  21.6 1.6 %collective-permute-start.3 = (f32[832,128]{1,0:T(8,128)S(1)}, f32[832,128]{1,0:T(8,128)S(1)}, u32[]{:S(2)}, u32[]{:S(2)}) collective-permute-start(f32[832,128]{1,0:T(8,128)S(1)} %get-tuple-element.92), channel_id=1, source_target_pairs={{0,4},{4,0},{8,12},{12,8},{16,20},{20,16},{24,28},{28,24},{1,5},{5... | collective-permute-start | bytes 1277960 | tf_op jit(solution)/shard_map/ppermute | solution.py:716
  23.1 3.0 %collective-permute-start.2 = (f32[832,128]{1,0:T(8,128)S(1)}, f32[832,128]{1,0:T(8,128)S(1)}, u32[]{:S(2)}, u32[]{:S(2)}) collective-permute-start(f32[832,128]{1,0:T(8,128)S(1)} %get-tuple-element.90.refs_13_), channel_id=1, source_target_pairs={{4,8},{8,4},{12,16},{16,12},{20,24},{24,20},{5,9},{9,5},{13,17},{1... | collective-permute-start | bytes 1277960 | tf_op jit(solution)/shard_map/ppermute | solution.py:716
  26.2 4.2 %shard_map.76 = (f32[4,2,304,128]{3,2,1,0:T(8,128)S(1)}, f32[2,2,288,128]{3,2,1,0:T(8,128)S(1)}, f32[17,144,128]{2,1,0:T(8,128)S(1)}, f32[7,2,144,128]{3,2,1,0:T(8,128)S(1)}, f32[4,144,128]{2,1,0:T(8,128)S(1)}) custom-call(s32[8]{0:T(128)S(1)} %concatenate.3.meta, f32[2]{0:T(128)S(1)} %copy-done.4, f32[4,2,304,128]{3,2,1,0:T(8,128)S(1)} %get-tuple-element.77.refs_0_.res, ...), custom_call_target="tpu_custom_call" | custom-call | flops 1 | bytes 1 | tf_op jit(solution)/shard_map/pallas_call | solution.py:692
  30.4 0.9 %collective-permute-done.4.xod = f32[4,256,256]{2,1,0:T(8,128)S(1)} collective-permute-done((f32[4,256,256]{2,1,0:T(8,128)}, f32[4,256,256]{2,1,0:T(8,128)S(1)}, u32[]{:S(2)}, u32[]{:S(2)}) %collective-permute-start.4) | collective-permute-done | bytes 1048608 | tf_op jit(solution)/shard_map/ppermute | solution.py:716
  31.3 1.0 %copy-done.2 = f32[4,256,256]{2,1,0:T(8,128)} copy-done((f32[4,256,256]{2,1,0:T(8,128)}, f32[4,256,256]{2,1,0:T(8,128)S(1)}, u32[]{:S(2)}) %copy-start.2) | copy-done | bytes 1048600
  32.3 0.0 collective-permute-done.5.xev
  32.3 1.2 %copy-done.3 = f32[4,256,256]{2,1,0:T(8,128)S(1)} copy-done((f32[4,256,256]{2,1,0:T(8,128)S(1)}, f32[4,256,256]{2,1,0:T(8,128)}, u32[]{:S(2)}) %copy-start.3) | copy-done | bytes 1048600
  33.5 4.2 %shard_map.78 = (f32[4,2,304,128]{3,2,1,0:T(8,128)S(1)}, f32[4,2,304,128]{3,2,1,0:T(8,128)S(1)}, f32[4,2,288,128]{3,2,1,0:T(8,128)S(1)}, f32[2,2,304,128]{3,2,1,...) custom-call(s32[8]{0:T(128)S(1)} %concatenate.3.meta, ...), custom_call_target="tpu_custom_call" | custom-call | flops 1 | bytes 1 | tf_op jit(solution)/shard_map/pallas_call | solution.py:692
  37.7 0.0 collective-permute-done.3.sev
  37.7 2.7 %collective-permute-done.2.sod = f32[832,128]{1,0:T(8,128)S(1)} collective-permute-done((f32[832,128]{1,0:T(8,128)S(1)}, f32[832,128]{1,0:T(8,128)S(1)}, u32[]{:S(2)}, u32[]{:S(2)}) %collective-permute-start.2) | collective-permute-done | bytes 426016 | tf_op jit(solution)/shard_map/ppermute | solution.py:716
  40.4 5.5 %shard_map.79 = (f32[4,2,304,128]{3,2,1,0:T(8,128)S(1)}, f32[4,2,304,128]{3,2,1,0:T(8,128)S(1)}, f32[4,2,288,128]{3,2,1,0:T(8,128)S(1)}, f32[2,2,304,128]{3,2,1,...) custom-call(s32[8]{0:T(128)S(1)} %concatenate.3.meta, ...), custom_call_target="tpu_custom_call", output_to_operand_aliasing={{0}: (17, {}), {1}: (18, {}), {2}: (19, {}), {3}: (20, {}),... | custom-call | flops 1 | bytes 1 | tf_op jit(solution)/shard_map/pallas_call | solution.py:692
  46.0 2.8 %collective-permute-start.6 = (f32[3,144,128]{2,1,0:T(8,128)S(1)}, f32[3,144,128]{2,1,0:T(8,128)S(1)}, u32[]{:S(2)}, u32[]{:S(2)}) collective-permute-start(f32[3,144,128]{2,1,0:T(8,128)S(1)} %get-tuple-element.109), channel_id=1, source_target_pairs={{4,8},{8,4},{12,16},{16,12},{20,24},{24,20},{5,9},{9,5},{13,17},{1... | collective-permute-start | bytes 663560 | tf_op jit(solution)/shard_map/ppermute | solution.py:716
  48.8 0.1 collective-permute-start.7
  48.9 3.6 %collective-permute-start.10 = (f32[2,288,128]{2,1,0:T(8,128)S(1)}, f32[2,288,128]{2,1,0:T(8,128)S(1)}, u32[]{:S(2)}, u32[]{:S(2)}) collective-permute-start(f32[2,288,128]{2,1,0:T(8,128)S(1)} %get-tuple-element.114), channel_id=1, source_target_pairs={{4,8},{8,4},{12,16},{16,12},{20,24},{24,20},{5,9},{9,5},{13,17},{1... | collective-permute-start | bytes 884744 | tf_op jit(solution)/shard_map/ppermute | solution.py:716
  52.5 0.1 collective-permute-start.11
  52.6 3.9 %collective-permute-done.6.rod = f32[3,144,128]{2,1,0:T(8,128)S(1)} collective-permute-done((f32[3,144,128]{2,1,0:T(8,128)S(1)}, f32[3,144,128]{2,1,0:T(8,128)S(1)}, u32[]{:S(2)}, u32[]{:S(2)}) %collective-permute-start.6) | collective-permute-done | bytes 221216 | tf_op jit(solution)/shard_map/ppermute | solution.py:716
  56.5 0.0 collective-permute-done.7.rev
  56.5 1.1 %shard_map.80 = (f32[4,144,128]{2,1,0:T(8,128)S(1)}, f32[2,144,128]{2,1,0:T(8,128)S(1)}, f32[2,144,128]{2,1,0:T(8,128)S(1)}) custom-call(s32[8]{0:T(128)S(1)} %concatenate.3.meta, f32[7,2,144,128]{3,2,1,0:T(8,128)S(1)} %get-tuple-element.91.gci, f32[6,2,144,128]{3,2,1,0:T(8,128)S(1)} %get-tuple-element.107.gco, f32[4,144,128]{2,1,0:T(8,128)S(1)} %get-tuple-element.108.base, ...), custom_call_target="tpu_custom_call" | custom-call | flops 1 | bytes 1 | tf_op jit(solution)/shard_map/pallas_call | solution.py:692
  57.6 2.1 %collective-permute-start.8 = (f32[2,144,128]{2,1,0:T(8,128)S(1)}, f32[2,144,128]{2,1,0:T(8,128)S(1)}, u32[]{:S(2)}, u32[]{:S(2)}) collective-permute-start(f32[2,144,128]{2,1,0:T(8,128)S(1)} %get-tuple-element.112), channel_id=1, source_target_pairs={{4,8},{8,4},{12,16},{16,12},{20,24},{24,20},{5,9},{9,5},{13,17},{1... | collective-permute-start | bytes 442376 | tf_op jit(solution)/shard_map/ppermute | solution.py:716
  59.8 0.1 collective-permute-start.9
  59.8 3.0 %collective-permute-done.10.vod = f32[2,288,128]{2,1,0:T(8,128)S(1)} collective-permute-done((f32[2,288,128]{2,1,0:T(8,128)S(1)}, f32[2,288,128]{2,1,0:T(8,128)S(1)}, u32[]{:S(2)}, u32[]{:S(2)}) %collective-permute-start.10) | collective-permute-done | bytes 294944 | tf_op jit(solution)/shard_map/ppermute | solution.py:716
  62.8 0.0 collective-permute-done.11.vev
  62.8 2.3 %collective-permute-done.8.tod = f32[2,144,128]{2,1,0:T(8,128)S(1)} collective-permute-done((f32[2,144,128]{2,1,0:T(8,128)S(1)}, f32[2,144,128]{2,1,0:T(8,128)S(1)}, u32[]{:S(2)}, u32[]{:S(2)}) %collective-permute-start.8) | collective-permute-done | bytes 147488 | tf_op jit(solution)/shard_map/ppermute | solution.py:716
  65.1 0.0 collective-permute-done.9.tev
  65.1 6.7 %shard_map.81 = f32[8,256,256]{2,1,0:T(8,128)} custom-call(s32[8]{0:T(128)S(1)} %concatenate.3.meta, f32[2]{0:T(128)S(1)} %copy-done.4, f32[7,2,144,128]{3,2,1,0:T(8,128)S(1)} %get-tuple-element.91.gci, f32[6,2,144,128]{3,2,1,0:T(8,128)S(1)} %get-tuple-element.107.gco, f32[4,144,128]{2,1,0:T(8,128)S(1)} %get-tuple-element.108.base, ...), custom_call_target="tpu_custom_call" | custom-call | flops 1 | bytes 1 | tf_op jit(solution)/shard_map/pallas_call | solution.py:692
  (6 shorter events, 0.0 us)
Async XLA Ops:
  2.9 28.4 %collective-permute-start.4 = (f32[4,256,256]{2,1,0:T(8,128)}, f32[4,256,256]{2,1,0:T(8,128)S(1)}, u32[]{:S(2)}, u32[]{:S(2)}) collective-permute-start(f32[4,256,256]{2,1,0:T(8,128)} %get-tuple-element.97), channel_id=1, source_target_pairs={{4,8},{8,4},{12,16},{16,12},{20,24},{24,20},{5,9},{9,5},{13,17},{1... | collective-permute-start | bytes 3145736 | tf_op jit(solution)/shard_map/ppermute | solution.py:716
  6.6 5.5 %copy-start.5 = (s32[2]{0:T(128)S(1)}, s32[2]{0:T(128)}, u32[]{:S(2)}) copy-start(s32[2]{0:T(128)} %param.11) | copy-start | bytes 28
  6.6 5.5 %copy-start.6 = (s32[2]{0:T(128)S(1)}, s32[2]{0:T(128)}, u32[]{:S(2)}) copy-start(s32[2]{0:T(128)} %param.10) | copy-start | bytes 28
  6.6 5.6 %copy-start.7 = (s32[2]{0:T(128)S(1)}, s32[2]{0:T(128)}, u32[]{:S(2)}) copy-start(s32[2]{0:T(128)} %param.12) | copy-start | bytes 28
  6.6 5.7 %copy-start.8 = (f32[8]{0:T(128)S(1)}, f32[8]{0:T(128)}, u32[]{:S(2)}) copy-start(f32[8]{0:T(128)} %param.9) | copy-start | bytes 100
  6.6 5.6 %copy-start = (f32[8,256,256]{2,1,0:T(8,128)S(1)}, f32[8,256,256]{2,1,0:T(8,128)}, u32[]{:S(2)}) copy-start(f32[8,256,256]{2,1,0:T(8,128)} %pot.5) | copy-start | bytes 6291460
  6.6 5.6 %copy-start.4 = (f32[2]{0:T(128)S(1)}, f32[2]{0:T(128)}, u32[]{:S(2)}) copy-start(f32[2]{0:T(128)} %cur.11) | copy-start | bytes 28
  6.7 25.6 %collective-permute-start.5 = (f32[4,256,256]{2,1,0:T(8,128)}, f32[4,256,256]{2,1,0:T(8,128)}, u32[]{:S(2)}, u32[]{:S(2)}) collective-permute-start(f32[4,256,256]{2,1,0:T(8,128)} %get-tuple-element.98), channel_id=1, source_target_pairs={{0,4},{4,0},{8,12},{12,8},{16,20},{20,16},{24,28},{28,24},{1,5},{5... | collective-permute-start | bytes 3145736 | tf_op jit(solution)/shard_map/ppermute | solution.py:716
  8.8 10.6 %collective-permute-start = (f32[2,8,16,256]{3,2,1,0:T(8,128)}, f32[2,8,16,256]{3,2,1,0:T(8,128)S(1)}, u32[]{:S(2)}, u32[]{:S(2)}) collective-permute-start(f32[2,8,16,256]{3,2,1,0:T(8,128)} %get-tuple-element.62), channel_id=1, source_target_pairs={{1,2},{2,1},{5,6},{6,5},{9,10},{10,9},{13,14},{14,13},{17,18},{18,... | collective-permute-start | bytes 786440 | tf_op jit(solution)/shard_map/ppermute | solution.py:716
  12.0 7.6 %collective-permute-start.1 = (f32[2,8,16,256]{3,2,1,0:T(8,128)}, f32[2,8,16,256]{3,2,1,0:T(8,128)}, u32[]{:S(2)}, u32[]{:S(2)}) collective-permute-start(f32[2,8,16,256]{3,2,1,0:T(8,128)} %get-tuple-element.63), channel_id=1, source_target_pairs={{0,1},{1,0},{2,3},{3,2},{4,5},{5,4},{6,7},{7,6},{8,9},{9,8},{10,11... | collective-permute-start | bytes 786440 | tf_op jit(solution)/shard_map/ppermute | solution.py:716
  12.3 1.6 %copy-start.1 = (s32[8,256,256]{2,1,0:T(8,128)S(1)}, s32[8,256,256]{2,1,0:T(8,128)}, u32[]{:S(2)}) copy-start(s32[8,256,256]{2,1,0:T(8,128)} %cls.5) | copy-start | bytes 6291460
  21.6 16.2 %collective-permute-start.3 = (f32[832,128]{1,0:T(8,128)S(1)}, f32[832,128]{1,0:T(8,128)S(1)}, u32[]{:S(2)}, u32[]{:S(2)}) collective-permute-start(f32[832,128]{1,0:T(8,128)S(1)} %get-tuple-element.92), channel_id=1, source_target_pairs={{0,4},{4,0},{8,12},{12,8},{16,20},{20,16},{24,28},{28,24},{1,5},{5... | collective-permute-start | bytes 1277960 | tf_op jit(solution)/shard_map/ppermute | solution.py:716
  23.1 17.3 %collective-permute-start.2 = (f32[832,128]{1,0:T(8,128)S(1)}, f32[832,128]{1,0:T(8,128)S(1)}, u32[]{:S(2)}, u32[]{:S(2)}) collective-permute-start(f32[832,128]{1,0:T(8,128)S(1)} %get-tuple-element.90.refs_13_), channel_id=1, source_target_pairs={{4,8},{8,4},{12,16},{16,12},{20,24},{24,20},{5,9},{9,5},{13,17},{1... | collective-permute-start | bytes 1277960 | tf_op jit(solution)/shard_map/ppermute | solution.py:716
  31.3 1.0 %copy-start.2 = (f32[4,256,256]{2,1,0:T(8,128)}, f32[4,256,256]{2,1,0:T(8,128)S(1)}, u32[]{:S(2)}) copy-start(f32[4,256,256]{2,1,0:T(8,128)S(1)} %collective-permute-done.4.xod) | copy-start | bytes 3145732
  32.3 1.2 %copy-start.3 = (f32[4,256,256]{2,1,0:T(8,128)S(1)}, f32[4,256,256]{2,1,0:T(8,128)}, u32[]{:S(2)}) copy-start(f32[4,256,256]{2,1,0:T(8,128)} %copy-done.2) | copy-start | bytes 3145732
  46.0 10.5 %collective-permute-start.6 = (f32[3,144,128]{2,1,0:T(8,128)S(1)}, f32[3,144,128]{2,1,0:T(8,128)S(1)}, u32[]{:S(2)}, u32[]{:S(2)}) collective-permute-start(f32[3,144,128]{2,1,0:T(8,128)S(1)} %get-tuple-element.109), channel_id=1, source_target_pairs={{4,8},{8,4},{12,16},{16,12},{20,24},{24,20},{5,9},{9,5},{13,17},{1... | collective-permute-start | bytes 663560 | tf_op jit(solution)/shard_map/ppermute | solution.py:716
  48.8 7.7 %collective-permute-start.7 = (f32[3,144,128]{2,1,0:T(8,128)S(1)}, f32[3,144,128]{2,1,0:T(8,128)S(1)}, u32[]{:S(2)}, u32[]{:S(2)}) collective-permute-start(f32[3,144,128]{2,1,0:T(8,128)S(1)} %get-tuple-element.110), channel_id=1, source_target_pairs={{0,4},{4,0},{8,12},{12,8},{16,20},{20,16},{24,28},{28,24},{1,5},{5... | collective-permute-start | bytes 663560 | tf_op jit(solution)/shard_map/ppermute | solution.py:716
  48.9 13.9 %collective-permute-start.10 = (f32[2,288,128]{2,1,0:T(8,128)S(1)}, f32[2,288,128]{2,1,0:T(8,128)S(1)}, u32[]{:S(2)}, u32[]{:S(2)}) collective-permute-start(f32[2,288,128]{2,1,0:T(8,128)S(1)} %get-tuple-element.114), channel_id=1, source_target_pairs={{4,8},{8,4},{12,16},{16,12},{20,24},{24,20},{5,9},{9,5},{13,17},{1... | collective-permute-start | bytes 884744 | tf_op jit(solution)/shard_map/ppermute | solution.py:716
  52.5 10.3 %collective-permute-start.11 = (f32[2,288,128]{2,1,0:T(8,128)S(1)}, f32[2,288,128]{2,1,0:T(8,128)S(1)}, u32[]{:S(2)}, u32[]{:S(2)}) collective-permute-start(f32[2,288,128]{2,1,0:T(8,128)S(1)} %get-tuple-element.115), channel_id=1, source_target_pairs={{0,4},{4,0},{8,12},{12,8},{16,20},{20,16},{24,28},{28,24},{1,5},{5... | collective-permute-start | bytes 884744 | tf_op jit(solution)/shard_map/ppermute | solution.py:716
  57.6 7.5 %collective-permute-start.8 = (f32[2,144,128]{2,1,0:T(8,128)S(1)}, f32[2,144,128]{2,1,0:T(8,128)S(1)}, u32[]{:S(2)}, u32[]{:S(2)}) collective-permute-start(f32[2,144,128]{2,1,0:T(8,128)S(1)} %get-tuple-element.112), channel_id=1, source_target_pairs={{4,8},{8,4},{12,16},{16,12},{20,24},{24,20},{5,9},{9,5},{13,17},{1... | collective-permute-start | bytes 442376 | tf_op jit(solution)/shard_map/ppermute | solution.py:716
  59.8 5.4 %collective-permute-start.9 = (f32[2,144,128]{2,1,0:T(8,128)S(1)}, f32[2,144,128]{2,1,0:T(8,128)S(1)}, u32[]{:S(2)}, u32[]{:S(2)}) collective-permute-start(f32[2,144,128]{2,1,0:T(8,128)S(1)} %get-tuple-element.113), channel_id=1, source_target_pairs={{0,4},{4,0},{8,12},{12,8},{16,20},{20,16},{24,28},{28,24},{1,5},{5... | collective-permute-start | bytes 442376 | tf_op jit(solution)/shard_map/ppermute | solution.py:716

commit v2 on v1

v2 whole, which is shorter than its diff:
```python
import functools

import jax
import jax.numpy as jnp
from jax import lax
from jax.experimental import pallas as pl
from jax.experimental.pallas import tpu as pltpu
from jax.sharding import PartitionSpec as P

OMEGA = 0.8
HALO = 16
CORNER = 12
GROUP = 4
TRIM = 8
STEP = 16
PAD = 8
LANES = 128
F32 = jnp.float32
XL, XU, YL, YU, ZL, ZU = range(6)

VM = pl.BlockSpec(memory_space=pltpu.VMEM)
SM = pl.BlockSpec(memory_space=pltpu.SMEM)


class Dims:
    def __init__(self, shape):
        self.rows, self.cols, self.depth = shape
        self.halves = self.depth // LANES
        self.ext = self.cols + 2 * HALO
        self.padded = self.ext + 2 * PAD
        self.crows = self.rows // 2
        self.cext = self.ext // 2
        self.whole = [(0, self.ext)]
        side = HALO + PAD
        self.inside = [(side, self.ext - 2 * side)]
        self.strips = [(0, side), (self.ext - side, side)]

    def within(self, margin):
        return [(margin, self.ext - 2 * margin)]

    def beside(self, margin):
        return [(0, margin), (self.ext - margin, margin)]


def lanes_of(rows):
    return lax.broadcasted_iota(jnp.int32, (rows, LANES), 1)


def below(parts):
    return [pltpu.roll(parts[1], 1, 1), parts[0]]


def above(parts):
    return [parts[1], pltpu.roll(parts[0], LANES - 1, 1)]


def depth_shuffle(depth, back=False):
    left = lax.broadcasted_iota(jnp.int32, (depth, depth), 0)
    right = lax.broadcasted_iota(jnp.int32, (depth, depth), 1)
    if back:
        left, right = right, left
    target = jnp.where(left % 2 == 0, left // 2, depth // 2 + left // 2)
    return jnp.where(right == target, 1.0, 0.0).astype(jnp.bfloat16)


def face(total):
    return jnp.where(total > 0, 2.0 / total, 0.0)


def lookup(cells, table):
    bits = [(cells & (1 << b)) != 0 for b in range(3)]
    level = [table[k] for k in range(8)]
    for bit in bits:
        level = [jnp.where(bit, level[k + 1], level[k]) for k in range(0, len(level), 2)]
    return level[0]


def sweep(dims, get, targets, weights, out, scale=None, regions=None):
    for y0, size in regions or dims.whole:
        for at in range(y0, y0 + size, STEP):
            width = min(STEP, y0 + size - at)
            span, wide = pl.ds(at, width), pl.ds(at + PAD, width)
            held = {}

            def value(x):
                if x not in held:
                    held[x] = [get(x)[h, wide, :] for h in range(dims.halves)]
                return held[x]

            for x in targets:
                here, w = value(x), weights(x)
                zlow, zhigh = below(here), above(here)
                for h in range(dims.halves):
                    acc = w[XL][h, span, :] * value(x - 1)[h]
                    acc += w[XU][h, span, :] * value(x + 1)[h]
                    acc += w[YL][h, span, :] * get(x)[h, pl.ds(at + PAD - 1, width), :]
                    acc += w[YU][h, span, :] * get(x)[h, pl.ds(at + PAD + 1, width), :]
                    acc += w[ZL][h, span, :] * zlow[h]
                    acc += w[ZU][h, span, :] * zhigh[h]
                    if scale is None:
                        out(x)[h, wide, :] = acc + (1.0 - OMEGA) * here[h]
                    else:
                        out(x)[h, span, :] = (acc - OMEGA * here[h]) * scale(x)[h, span, :]


def sources(dims, meta, cur, count, targets, fix, regions=None):
    spots = []
    anywhere = None
    for s in range(count):
        row, ext_col = meta[s], meta[count + s] + HALO
        held = None
        for y0, size in regions or dims.whole:
            hit = (ext_col >= y0) & (ext_col < y0 + size)
            held = hit if held is None else held | hit
        held = (row >= targets[0]) & (row <= targets[-1]) & held
        anywhere = held if anywhere is None else anywhere | held
        spots.append((s, row, ext_col, held))

    @pl.when(anywhere)
    def _():
        for s, row, ext_col, held in spots:
            for x in targets:

                @pl.when(held & (row == x))
                def _(s=s, ext_col=ext_col, x=x):
                    for h in range(dims.halves):
                        hit = 2 * lanes_of(1) + h == meta[2 * count + s]
                        fix(x, ext_col, h, jnp.where(hit, cur[s], 0.0))


def add_swept(field, scale, col, h, amount):
    field[h, pl.ds(col + PAD, 1), :] += amount / scale[h, pl.ds(col, 1), :]


def row_faces(dims, row, row_below, yl_out, zl_out, xl_out, regions=None):
    for y0, size in regions or dims.whole:
        span, wide = pl.ds(y0, size), pl.ds(y0 + PAD, size)
        here = [row[h, wide, :] for h in range(dims.halves)]
        zlow = below(here)
        zlow[0] = jnp.where(lanes_of(size) == 0, 0.0, zlow[0])
        for h in range(dims.halves):
            if xl_out is not None:
                xl_out[h, span, :] = face(here[h] + row_below[h, wide, :])
            if yl_out is not None:
                yl_out[h, wide, :] = face(here[h] + row[h, pl.ds(y0 + PAD - 1, size), :])
                zl_out[h, span, :] = face(here[h] + zlow[h])


def row_weights(dims, row, xl, xu, yl, zl, weights, scale, regions=None):
    for y0, size in regions or dims.whole:
        span, wide = pl.ds(y0, size), pl.ds(y0 + PAD, size)
        low = [zl[h, span, :] for h in range(dims.halves)]
        high = above(low)
        lane = lanes_of(size)
        top = dims.halves - 1
        high[top] = jnp.where(lane == LANES - 1, face(row[top, wide, :]), high[top])
        for h in range(dims.halves):
            parts = [
                xl[h, span, :],
                xu[h, span, :],
                yl[h, wide, :],
                yl[h, pl.ds(y0 + PAD + 1, size), :],
                low[h],
                high[h],
            ]
            diag = parts[0] + parts[1] + parts[2] + parts[3] + parts[4] + parts[5]
            gain = jnp.where(row[h, wide, :] > 0, OMEGA / diag, 0.0)
            scale[h, span, :] = diag * (1.0 / OMEGA)
            if h == 0:
                parts[ZL] = jnp.where(lane == 0, 0.0, parts[ZL])
            if h == top:
                parts[ZU] = jnp.where(lane == LANES - 1, 0.0, parts[ZU])
            for k in range(6):
                weights[k][h, span, :] = gain * parts[k]


def split_dot(field, chosen, pieces=2):
    total = None
    for _ in range(pieces):
        piece = field.astype(jnp.bfloat16)
        field = field - piece.astype(F32)
        term = jnp.dot(piece, chosen, preferred_element_type=F32)
        total = term if total is None else total + term
    return total


def restrict(dims, rows, offset, parities, parts=(0, 1)):
    total = None
    for h in parts:
        for row in rows:
            for parity in parities:
                part = row[h, pl.ds(offset + parity, dims.cext, stride=2), :]
                total = part if total is None else total + part
    return total


def edge_message(axis, dim, width, wanted, pot, cls, out, kept, sems):
    high = lax.axis_index(axis) % 2 == wanted
    start = jnp.where(high, pot.shape[dim] - width, 0)
    if dim == 0:
        at, pot_out, cls_out = pl.ds(start, width), out.at[pl.ds(0, width)], pl.ds(width, width)
    else:
        at = (slice(None), pl.ds(pl.multiple_of(start, 8), width))
        pot_out, cls_out = out.at[0], 1
    copies = [
        pltpu.make_async_copy(cls.at[at], kept, sems.at[0]),
        pltpu.make_async_copy(pot.at[at], pot_out, sems.at[1]),
    ]
    for copy in copies:
        copy.start()
    copies[0].wait()
    out[cls_out] = kept[...].astype(F32) + 1.0
    copies[1].wait()


def tile_rows(dims, refs):
    rows = dims.rows
    ends, pairs = [0, rows - 1], [0, 1, rows - 2, rows - 1]
    edges = [pairs, pairs, [1, rows - 1], ends, ends]

    def getter(edge, middle, named, first):
        others = [x for x in range(first, rows) if x not in named]
        return lambda x: edge.at[named.index(x)] if x in named else middle.at[others.index(x)]

    found = [getter(refs[k], refs[5 + k], edges[k], int(k == 2)) for k in range(5)]
    return found + list(refs[10:13])


def own_rows(dims, nsrc, meta, cur, res, vol, fx, fy, fz, wts, scl, one, regions, face_regions):
    rows = dims.rows
    for x in range(rows):
        row_faces(
            dims,
            res(x),
            res(x - 1) if x else None,
            fy(x),
            fz(x),
            fx(x) if x else None,
            face_regions,
        )
    weights = lambda x: [wts.at[k, x - 1] for k in range(6)]
    for x in range(1, rows - 1):
        row_weights(
            dims, res(x), fx(x), fx(x + 1), fy(x), fz(x), weights(x),
            scl.at[x - 1], regions,
        )
    sweep(dims, vol, range(1, rows - 1), weights, lambda x: one.at[x - 1], regions=regions)
    sources(
        dims, meta, cur, nsrc, range(1, rows - 1),
        lambda x, *rest: add_swept(one.at[x - 1], scl.at[x - 1], *rest),
        regions,
    )


def tile_kernel(dims, nsrc, meta, cur, table, pot, cls, *refs):
    res, vol, fx, fy, fz, wts, scl, one = tile_rows(dims, refs)
    margin = PAD + HALO
    shuffle = depth_shuffle(dims.depth)
    for x in range(dims.rows):
        field = split_dot(pot[x], shuffle)
        number = split_dot(cls[x].astype(F32), shuffle, 1).astype(jnp.int32)
        for h in range(dims.halves):
            lanes = slice(h * LANES, (h + 1) * LANES)
            zero = jnp.zeros((margin, LANES), F32)
            for ref in (res, vol):
                ref(x)[h, pl.ds(0, margin), :] = zero
                ref(x)[h, pl.ds(margin + dims.cols, margin), :] = zero
            vol(x)[h, pl.ds(margin, dims.cols), :] = field[:, lanes]
            res(x)[h, pl.ds(margin, dims.cols), :] = lookup(number[:, lanes], table)
    own_rows(dims, nsrc, meta, cur, res, vol, fx, fy, fz, wts, scl, one, dims.inside,
             [(HALO, dims.cols)])


def strip_kernel(dims, nsrc, meta, cur, table, yod, yev, *refs):
    count = len(dims.tile)
    res_edge, vol_edge = refs[count], refs[count + 1]
    res, vol, fx, fy, fz, wts, scl, one = tile_rows(dims, refs[count : 2 * count])
    send_od, send_ev = refs[2 * count :]
    rows, halves, cols = dims.rows, dims.halves, dims.cols
    odd_x, odd_y = meta[3 * nsrc] == 1, meta[3 * nsrc + 1] == 1
    shuffle = depth_shuffle(dims.depth)
    for into, take_ev in ((PAD, True), (PAD + HALO + cols, False)):
        pair = []
        for k in range(2):
            a, b = yod[k], yev[k]
            chosen = jnp.where(odd_y, b, a) if take_ev else jnp.where(odd_y, a, b)
            chosen = chosen.reshape(rows * HALO, dims.depth)
            pair.append(split_dot(chosen, shuffle, 1 if k else 2))
        number = pair[1].astype(jnp.int32)
        inverse = jnp.where(number > 0, lookup(number - 1, table), 0.0)
        for x in range(rows):
            at = slice(x * HALO, (x + 1) * HALO)
            for h in range(halves):
                lanes = slice(h * LANES, (h + 1) * LANES)
                vol(x)[h, pl.ds(into, HALO), :] = pair[0][at, lanes]
                res(x)[h, pl.ds(into, HALO), :] = inverse[at, lanes]
    for x in range(rows):
        for h in range(halves):
            fy(x)[h, pl.ds(PAD + dims.ext, PAD), :] = jnp.zeros((PAD, LANES), F32)
    own_rows(dims, nsrc, meta, cur, res, vol, fx, fy, fz, wts, scl, one, dims.strips, dims.strips)

    def fill(send, high):
        edge = jnp.where(high, 2, 0)
        inner = jnp.where(high, rows - 2, 1)
        for h in range(halves):
            send[pl.ds(h * dims.ext, dims.ext), :] = one[inner - 1, h, pl.ds(PAD, dims.ext), :]
        base = halves * dims.ext
        for k in range(4):
            ref = vol_edge if k < 2 else res_edge
            for h in range(halves):
                at = base + (k * halves + h) * 2 * CORNER
                send[pl.ds(at, CORNER), :] = ref[
                    edge + k % 2, h, pl.ds(PAD + HALO - CORNER, CORNER), :
                ]
                send[pl.ds(at + CORNER, CORNER), :] = ref[
                    edge + k % 2, h, pl.ds(PAD + HALO + cols, CORNER), :
                ]

    fill(send_od, odd_x)
    fill(send_ev, jnp.logical_not(odd_x))


def first_kernel(dims, nsrc, meta, cur, *refs):
    res, vol, fx, fy, fz, wts, scl, one = tile_rows(dims, refs[: len(dims.tile)])
    two, rsd, ced, gco, ins, cfc = refs[len(dims.tile) + 1 :]
    rows, halves = dims.rows, dims.halves
    weights = lambda x: [wts.at[k, x - 1] for k in range(6)]
    sweep(
        dims, lambda x: one.at[x - 1], range(2, rows - 2), weights, lambda x: two.at[x - 2]
    )

    sources(
        dims, meta, cur, nsrc, range(2, rows - 2),
        lambda x, *rest: add_swept(two.at[x - 2], scl.at[x - 1], *rest),
    )

    sweep(
        dims, lambda x: two.at[x - 2], range(3, rows - 3), weights, lambda x: rsd.at[x - 3],
        lambda x: scl.at[x - 1],
    )

    def fix_rsd(row, col, h, amount):
        rsd[row - 3, h, pl.ds(col, 1), :] += amount

    sources(dims, meta, cur, nsrc, range(3, rows - 3), fix_rsd)

    n = dims.crows
    for c in range(n):
        pair = lambda row: [row(2 * c), row(2 * c + 1)]
        if c:
            cfc[c] = restrict(dims, [fx(2 * c)], 0, (0, 1))
        cfc[n + 1 + c] = restrict(dims, pair(fy), PAD, (0,))
        cfc[2 * n + 1 + c] = restrict(dims, pair(fz), 0, (0, 1), (0,))
        top = None
        for row in pair(res):
            for parity in (0, 1):
                part = face(row[halves - 1, pl.ds(PAD + parity, dims.cext, stride=2), :])
                top = part if top is None else top + part
        cfc[3 * n + 1 + c] = top
        ins[c] = res(2 * c)[0, pl.ds(PAD, dims.cext, stride=2), :]
    for c in range(1, n - 1):
        kinds = [cfc[c], cfc[c + 1]] + [cfc[j * n + 1 + c] for j in (1, 2, 3)]
        for k, part in enumerate(coarse_weights(dims, ins[c], *kinds)):
            gco[k, c - 1] = part
    for side, c in enumerate((0, n - 1)):
        ced[4 * side] = cfc[1 if c == 0 else n - 1]
        for k in range(3):
            ced[4 * side + 1 + k] = cfc[(k + 1) * n + 1 + c]


def coarse_weights(dims, inside, xl, xu, yl, zl, top):
    lane = lanes_of(dims.cext)
    yu = pltpu.roll(yl, dims.cext - 1, 0)
    zu = jnp.where(lane == LANES - 1, top, pltpu.roll(zl, LANES - 1, 1))
    diag = xl + xu + yl + yu + zl + zu
    gain = jnp.where(inside > 0, OMEGA / diag, 0.0)
    zl = jnp.where(lane == 0, 0.0, zl)
    zu = jnp.where(lane == LANES - 1, 0.0, zu)
    return [gain * part for part in (xl, xu, yl, yu, zl, zu)] + [gain]


def neighbours(rows):
    ext = rows.shape[0]
    return (
        pltpu.roll(rows, 1, 0),
        pltpu.roll(rows, ext - 1, 0),
        pltpu.roll(rows, 1, 1),
        pltpu.roll(rows, LANES - 1, 1),
    )


def coarse_side(field, base, weights):
    ylow, yhigh, zlow, zhigh = neighbours(field)
    return (
        (1.0 - OMEGA) * field
        + base
        + weights[YL] * ylow
        + weights[YU] * yhigh
        + weights[ZL] * zlow
        + weights[ZU] * zhigh
    )


def edge_sweep(dims, nsrc, meta, cur, res, vol, fx, fy, fz, hres, hvol, hfx, hfy, hfz, hwts, hscl,
               edge, regions, face_regions):
    rows = dims.rows
    last = rows - 1
    row_faces(dims, hres.at[1], hres.at[0], hfy.at[0], hfz.at[0], hfx.at[0], face_regions)
    row_faces(dims, res.at[0], hres.at[1], None, None, hfx.at[1], face_regions)
    row_faces(dims, hres.at[2], res.at[3], hfy.at[1], hfz.at[1], hfx.at[2], face_regions)
    row_faces(dims, hres.at[3], hres.at[2], None, None, hfx.at[3], face_regions)
    weights = lambda k: [hwts.at[j, k] for j in range(6)]
    for k, (row, xl, xu, yl, zl) in enumerate((
        (hres.at[1], hfx.at[0], hfx.at[1], hfy.at[0], hfz.at[0]),
        (res.at[0], hfx.at[1], fx.at[0], fy.at[0], fz.at[0]),
        (res.at[3], fx.at[1], hfx.at[2], fy.at[1], fz.at[1]),
        (hres.at[2], hfx.at[2], hfx.at[3], hfy.at[1], hfz.at[1]),
    )):
        row_weights(dims, row, xl, xu, yl, zl, weights(k), hscl.at[k], regions)
    index = {-1: 0, 0: 1, last: 2, rows: 3}

    def start(x):
        if x < 0:
            return hvol.at[x + 2]
        if x >= rows:
            return hvol.at[x - rows + 2]
        return vol.at[x if x <= 1 else x - last + 3]

    for pair in ((-1, 0), (last, rows)):
        sweep(
            dims, start, pair, lambda x: weights(index[x]), lambda x: edge.at[index[x] + 1],
            regions=regions,
        )
    sources(
        dims, meta, cur, nsrc, (-1, 0, last, rows),
        lambda x, *rest: add_swept(edge.at[index[x] + 1], hscl.at[index[x]], *rest),
        regions,
    )


def edge_rows(dims, wts, scl, one, two, rsd, hwts, hscl, edge, htwo, redge):
    last = dims.rows - 1
    outer = lambda x: x + 1 if x <= 0 else x - last + 2
    inner = lambda x: 1 <= x <= last - 1
    weights = lambda x: [
        wts.at[k, x - 1] if inner(x) else hwts.at[k, outer(x)] for k in range(6)
    ]
    scale = lambda x: scl.at[x - 1] if inner(x) else hscl.at[outer(x)]

    def swept(x):
        if x <= 0:
            return edge.at[x + 2]
        return one.at[x - 1] if x < last else edge.at[x - last + 3]

    def twice(x):
        if x <= 1:
            return htwo.at[x + 1]
        return two.at[x - 2] if x < last - 1 else htwo.at[x - last + 4]

    def resid(x):
        if x <= 2:
            return redge.at[x]
        return rsd.at[x - 3] if x < last - 2 else redge.at[x - last + 5]

    return weights, scale, swept, twice, resid


def second_sweep(dims, nsrc, meta, cur, targets, weights, scale, swept, twice, regions):
    sweep(dims, swept, targets, weights, twice, regions=regions)
    sources(
        dims, meta, cur, nsrc, targets,
        lambda x, *rest: add_swept(twice(x), scale(x), *rest), regions,
    )


def residual(dims, nsrc, meta, cur, targets, weights, scale, twice, resid, regions):
    sweep(dims, twice, targets, weights, resid, scale, regions)

    def fix(x, col, h, amount):
        resid(x)[h, pl.ds(col, 1), :] += amount

    sources(dims, meta, cur, nsrc, targets, fix, regions)


def edge_kernel(dims, nsrc, meta, cur, table, xod, xev, wts, scl, one, two, res, vol, fx, fy, fz,
                hres, hvol, hfx, hfy, hfz, hwts, hscl, edge, htwo, redge):
    halves, cols = dims.halves, dims.cols
    odd_x = meta[3 * nsrc] == 1
    margin = PAD + HALO
    shuffle = depth_shuffle(dims.depth)
    for side in range(2):
        choose = lambda a, b: jnp.where(odd_x, b, a) if side == 0 else jnp.where(odd_x, a, b)
        for k in range(2):
            field = split_dot(choose(xod[k], xev[k]), shuffle)
            number = split_dot(choose(xod[2 + k], xev[2 + k]), shuffle, 1).astype(jnp.int32)
            inverse = jnp.where(number > 0, lookup(number - 1, table), 0.0)
            for h in range(halves):
                lanes = slice(h * LANES, (h + 1) * LANES)
                zero = jnp.zeros((margin, LANES), F32)
                for ref in (hres, hvol):
                    ref[2 * side + k, h, pl.ds(0, margin), :] = zero
                    ref[2 * side + k, h, pl.ds(margin + cols, margin), :] = zero
                wide = pl.ds(margin, cols)
                hvol[2 * side + k, h, wide, :] = field[:, lanes]
                hres[2 * side + k, h, wide, :] = inverse[:, lanes]
        for h in range(halves):
            hfy[side, h, pl.ds(PAD + dims.ext, PAD), :] = jnp.zeros((PAD, LANES), F32)
    edge_sweep(dims, nsrc, meta, cur, res, vol, fx, fy, fz, hres, hvol, hfx, hfy, hfz, hwts, hscl,
               edge, dims.inside, [(HALO, cols)])
    weights, scale, swept, twice, resid = edge_rows(
        dims, wts, scl, one, two, None, hwts, hscl, edge, htwo, redge
    )
    last = dims.rows - 1
    second_sweep(
        dims, nsrc, meta, cur, (0, 1, last - 1, last), weights, scale, swept, twice,
        dims.within(32),
    )
    residual(
        dims, nsrc, meta, cur, (1, 2, last - 2, last - 1), weights, scale, twice, resid,
        dims.within(40),
    )


def second_kernel(dims, nsrc, meta, cur, sod, sev, wts, scl, one, two, rsd, res, vol, fx, fy, fz,
                  ced, gci, ins, *refs):
    rows, halves, cols = dims.rows, dims.halves, dims.cols
    hres, hvol, hfx, hfy, hfz, hwts, hscl, edge, htwo, redge, gco, base, c_od, c_ev, v_od, v_ev = (
        refs[10:]
    )
    odd_x = meta[3 * nsrc] == 1
    last = rows - 1
    for side in range(2):
        choose = lambda a, b: jnp.where(odd_x, b, a) if side == 0 else jnp.where(odd_x, a, b)
        for h in range(halves):
            for k in range(2):
                for ref, kind in ((hvol, k), (hres, 2 + k)):
                    strip = halves * dims.ext + (kind * halves + h) * 2 * CORNER
                    low = pl.ds(strip, CORNER)
                    high = pl.ds(strip + CORNER, CORNER)
                    ref[2 * side + k, h, pl.ds(PAD + HALO - CORNER, CORNER), :] = choose(
                        sod[low, :], sev[low, :]
                    )
                    ref[2 * side + k, h, pl.ds(PAD + HALO + cols, CORNER), :] = choose(
                        sod[high, :], sev[high, :]
                    )
            span = pl.ds(h * dims.ext, dims.ext)
            edge[5 * side, h, pl.ds(PAD, dims.ext), :] = choose(sod[span, :], sev[span, :])
    edge_sweep(dims, nsrc, meta, cur, res, vol, fx, fy, fz, hres, hvol, hfx, hfy, hfz, hwts, hscl,
               edge, dims.strips, dims.strips)

    weights, scale, swept, twice, resid_row = edge_rows(
        dims, wts, scl, one, two, rsd, hwts, hscl, edge, htwo, redge
    )
    second_sweep(
        dims, nsrc, meta, cur, (0, 1, last - 1, last), weights, scale, swept, twice,
        dims.beside(32),
    )
    second_sweep(
        dims, nsrc, meta, cur, (-1, rows), weights, scale, swept, twice, dims.whole
    )
    pick_od = jnp.where(odd_x, 3, 2)
    pick_ev = jnp.where(odd_x, 2, 3)
    for h in range(halves):
        v_od[h, :, :] = htwo[pick_od, h, pl.ds(PAD, dims.ext), :]
        v_ev[h, :, :] = htwo[pick_ev, h, pl.ds(PAD, dims.ext), :]

    residual(
        dims, nsrc, meta, cur, (1, 2, last - 2, last - 1), weights, scale, twice, resid_row,
        dims.beside(40),
    )
    residual(
        dims, nsrc, meta, cur, (0, last), weights, scale, twice, resid_row, dims.whole
    )

    n = dims.crows
    bottom = restrict(dims, [hfx.at[1]], 0, (0, 1))
    topmost = restrict(dims, [hfx.at[2]], 0, (0, 1))

    e1, gc = [], []
    for c in range(n):
        total = restrict(dims, [resid_row(2 * c), resid_row(2 * c + 1)], 0, (0, 1))
        if 0 < c < n - 1:
            parts = [gci[k, c - 1] for k in range(7)]
        else:
            at = 0 if c == 0 else 4
            xl, xu = (bottom, ced[0]) if c == 0 else (ced[4], topmost)
            parts = coarse_weights(dims, ins[c], xl, xu, *(ced[at + k] for k in (1, 2, 3)))
            for k in range(6):
                gco[k, 0 if c == 0 else 1] = parts[k]
        gc.append(parts)
        e1.append(parts[6] * total)
        base[c] = e1[c]

    low = (e1[0], coarse_side(e1[0], e1[0], gc[0]) + gc[0][XU] * e1[1], gc[0][XL])
    high = (
        e1[n - 1],
        coarse_side(e1[n - 1], e1[n - 1], gc[n - 1]) + gc[n - 1][XL] * e1[n - 2],
        gc[n - 1][XU],
    )
    for k in range(3):
        c_od[k] = jnp.where(odd_x, high[k], low[k])
        c_ev[k] = jnp.where(odd_x, low[k], high[k])


def coarse_row(dims, gci, gco, c):
    if 0 < c < dims.crows - 1:
        return [gci[k, c - 1] for k in range(6)]
    return [gco[k, 0 if c == 0 else 1] for k in range(6)]


def third_kernel(dims, nsrc, meta, gci, gco, base, rod, rev, e3, c_od, c_ev):
    n = dims.crows
    odd_x = meta[3 * nsrc] == 1
    low = [jnp.where(odd_x, rev[k], rod[k]) for k in range(3)]
    high = [jnp.where(odd_x, rod[k], rev[k]) for k in range(3)]
    gc = lambda c: coarse_row(dims, gci, gco, c)

    def coarse_sweep(field, under, over):
        out = []
        for c in range(n):
            w = gc(c)
            new = coarse_side(field[c], base[c], w)
            new += w[XL] * (field[c - 1] if c else under)
            new += w[XU] * (field[c + 1] if c < n - 1 else over)
            out.append(new)
        return out

    e1 = [base[c] for c in range(n)]
    e2 = coarse_sweep(e1, low[0], high[0])
    under = low[1] + low[2] * e1[0]
    over = high[1] + high[2] * e1[n - 1]
    out = coarse_sweep(e2, under, over)
    for c in range(n):
        e3[c] = out[c]
    w = gc(0)
    first = (out[0], coarse_side(out[0], base[0], w) + w[XU] * out[1])
    w = gc(n - 1)
    final = (out[n - 1], coarse_side(out[n - 1], base[n - 1], w) + w[XL] * out[n - 2])
    for k in range(2):
        c_od[k] = jnp.where(odd_x, final[k], first[k])
        c_ev[k] = jnp.where(odd_x, first[k], final[k])


def fourth_kernel(dims, nsrc, meta, cur, gci, gco, base, e3, rod, rev, tod, tev, vod, vev, wts, scl,
                  two, hwts, hscl, htwo, out, raised, zero, three, done, sems):
    rows, halves, cols = dims.rows, dims.halves, dims.cols
    n = dims.crows
    odd_x = meta[3 * nsrc] == 1
    below_of = lambda od, ev: jnp.where(odd_x, ev, od)
    above_of = lambda od, ev: jnp.where(odd_x, od, ev)
    field = [e3[c] for c in range(n)]
    under = below_of(tod[1], tev[1]) + below_of(rod[2], rev[2]) * field[0]
    over = above_of(tod[1], tev[1]) + above_of(rod[2], rev[2]) * field[n - 1]
    e4 = [under]
    for c in range(n):
        w = coarse_row(dims, gci, gco, c)
        new = coarse_side(field[c], base[c], w)
        new += w[XL] * (field[c - 1] if c else below_of(tod[0], tev[0]))
        new += w[XU] * (field[c + 1] if c < n - 1 else above_of(tod[0], tev[0]))
        e4.append(new)
    e4.append(over)
    for c in range(n + 2):
        raised[c, pl.ds(0, dims.cext, stride=2), :] = e4[c]
        raised[c, pl.ds(1, dims.cext, stride=2), :] = e4[c]

    last = rows - 1

    def twice(x):
        if x <= 1:
            return htwo.at[x + 1]
        return two.at[x - 2] if x < last - 1 else htwo.at[x - last + 4]

    outer = lambda x: x + 1 if x <= 0 else x - last + 2
    inner = lambda x: 1 <= x <= last - 1
    weights = lambda x: [
        wts.at[k, x - 1] if inner(x) else hwts.at[k, outer(x)] for k in range(6)
    ]
    scale = lambda x: scl.at[x - 1] if inner(x) else hscl.at[outer(x)]
    for x in range(-2, rows + 2):
        for h in range(halves):
            near = pl.ds(TRIM, dims.ext - 2 * TRIM)
            wide = pl.ds(PAD + TRIM, dims.ext - 2 * TRIM)
            if x == -2:
                value = below_of(vod[h, near, :], vev[h, near, :])
            elif x == rows + 1:
                value = above_of(vod[h, near, :], vev[h, near, :])
            else:
                value = twice(x)[h, wide, :]
            zero[x + 2, h, wide, :] = value + raised[(x + 2) // 2, near, :]
    sweep(
        dims, lambda x: zero.at[x + 2], range(-1, rows + 1), weights, lambda x: three.at[x + 1],
        regions=dims.within(TRIM),
    )
    sources(
        dims, meta, cur, nsrc, range(-1, rows + 1),
        lambda x, *rest: add_swept(three.at[x + 1], scale(x), *rest), dims.within(TRIM),
    )
    copies = []
    shuffle = depth_shuffle(dims.depth, True)
    groups = [range(at, min(at + GROUP, rows)) for at in range(0, rows, GROUP)]
    inside = pl.ds(PAD + HALO, cols)
    four = lambda x: zero.at[x + 2]
    for k, group in enumerate(groups + [()]):
        if k:
            for x in groups[k - 1]:
                field = jnp.concatenate([four(x)[h, inside, :] for h in range(halves)], axis=1)
                done[x] = split_dot(field, shuffle)
        if group:
            sweep(
                dims, lambda x: three.at[x + 1], group, weights, four, regions=[(HALO, cols)]
            )
        if k:
            for x in groups[k - 1]:
                copy = pltpu.make_async_copy(done.at[x], out.at[x], sems.at[x])
                copy.start()
                copies.append(copy)
        if group:
            sources(
                dims, meta, cur, nsrc, group,
                lambda x, *rest: add_swept(four(x), scale(x), *rest), [(HALO, cols)],
            )
    for copy in copies:
        copy.wait()


def call(kernel, outs, ins, specs, scratch=(), aliases=None, out_specs=None, limit=24, cost=1):
    return pl.pallas_call(
        kernel,
        out_shape=[jax.ShapeDtypeStruct(shape, F32) for shape in outs],
        in_specs=specs,
        out_specs=out_specs if out_specs is not None else [VM] * len(outs),
        scratch_shapes=list(scratch),
        input_output_aliases=aliases or {},
        compiler_params=pltpu.CompilerParams(vmem_limit_bytes=limit * 2**20),
        cost_estimate=pl.CostEstimate(flops=cost, bytes_accessed=cost, transcendentals=0),
    )(*ins)


def swaps(count):
    pairs = []
    for first in (1, 0):
        found = []
        for low in range(first, count - 1, 2):
            found += [(low, low + 1), (low + 1, low)]
        pairs.append(found)
    return pairs


def swap(od, ev, axis):
    odd_pairs, even_pairs = swaps(lax.axis_size(axis))
    return lax.ppermute(od, axis, odd_pairs), lax.ppermute(ev, axis, even_pairs)


def per_device(potential, classes, sigma_table, row_index, col_index, depth_index, currents):
    dims = Dims(potential.shape)
    rows, cols, depth = potential.shape
    halves, ext, padded, n, cext = dims.halves, dims.ext, dims.padded, dims.crows, dims.cext
    nsrc = row_index.shape[0]
    gx, gy = lax.axis_index("gx"), lax.axis_index("gy")
    odd_x, odd_y = gx % 2, gy % 2
    meta = jnp.concatenate(
        [
            row_index - gx * rows,
            col_index - gy * cols,
            depth_index,
            jnp.stack([odd_x, odd_y]),
        ]
    ).astype(jnp.int32)
    table = 1.0 / sigma_table

    bind = lambda kernel: functools.partial(kernel, dims, nsrc)
    wide = lambda k: (k, halves, padded, LANES)
    flat = lambda k: (k, halves, ext, LANES)
    send = (halves * ext + 4 * halves * 2 * CORNER, LANES)
    coarse = lambda *k: (*k, cext, LANES)
    vmem = lambda *shapes: [pltpu.VMEM(shape, F32) for shape in shapes]
    hbm = pl.BlockSpec(memory_space=pl.ANY)
    far = pl.BlockSpec(memory_space=pltpu.HBM)

    def edge(axis, dim, width, wanted, shape, kept):
        (out,) = call(
            functools.partial(edge_message, axis, dim, width, wanted), [shape],
            [potential, classes], [far] * 2,
            scratch=[pltpu.VMEM(kept, jnp.int32), pltpu.SemaphoreType.DMA((2,))],
            limit=54,
        )
        return out

    xod, xev = swap(
        *(edge("gx", 0, 2, k, (4, cols, depth), (2, cols, depth)) for k in (1, 0)), "gx"
    )
    yod, yev = swap(
        *(
            edge("gy", 1, HALO, k, (2, rows, HALO, depth), (rows, HALO, depth))
            for k in (1, 0)
        ),
        "gy",
    )
    tile = dims.tile = [
        wide(4), wide(4), flat(2), wide(2), flat(2), wide(rows - 4), wide(rows - 4),
        flat(rows - 3), wide(rows - 2), flat(rows - 2), (6, *flat(rows - 2)), flat(rows - 2),
        wide(rows - 2),
    ]
    parts = call(
        bind(tile_kernel), tile, [meta, currents, table, potential, classes],
        [SM] * 3 + [VM] * 2,
        limit=4,
    )
    parts = call(
        bind(strip_kernel),
        tile + [send, send],
        [meta, currents, table, yod, yev, *parts],
        [SM] * 3 + [VM] * (2 + len(tile)),
        aliases={5 + k: k for k in range(len(tile))},
        limit=4,
    )
    res, vol, fx, fy, fz = parts[:5]
    wts, scl, one, s_od, s_ev = parts[10:]
    sod, sev = swap(s_od, s_ev, "gx")
    (two, rsd, ced, gci, ins) = call(
        bind(first_kernel),
        [wide(rows - 4), flat(rows - 6), coarse(8), coarse(7, n - 2), coarse(n)],
        [meta, currents, *parts[: len(tile) + 1]],
        [SM] * 2 + [VM] * (len(tile) + 1),
        scratch=vmem(coarse(4 * n + 1)),
        limit=4,
    )
    held = [
        wide(4), wide(4), flat(4), wide(2), flat(2), (6, *flat(4)), flat(4), wide(6), wide(6),
        flat(6),
    ]
    edges = call(
        bind(edge_kernel),
        held,
        [meta, currents, table, xod, xev, wts, scl, one, two, res, vol, fx, fy, fz],
        [SM] * 3 + [VM] * 11,
        limit=3,
    )
    ins_of = [meta, currents, sod, sev, wts, scl, one, two, rsd, res, vol, fx, fy, fz, ced, gci, ins]
    outs = call(
        bind(second_kernel),
        held + [coarse(6, 2), coarse(n), coarse(3), coarse(3)] + [flat(1)[1:]] * 2,
        ins_of + list(edges),
        [SM] * 2 + [VM] * (len(ins_of) - 2 + len(held)),
        aliases={len(ins_of) + k: k for k in range(len(held))},
        limit=4,
    )
    hwts, hscl, htwo = outs[5], outs[6], outs[8]
    gco, base, c_od, c_ev, v_od, v_ev = outs[10:]
    rod, rev = swap(c_od, c_ev, "gx")
    vod, vev = swap(v_od, v_ev, "gx")
    (e3, t_od, t_ev) = call(
        bind(third_kernel),
        [coarse(n), coarse(2), coarse(2)],
        [meta, gci, gco, base, rod, rev],
        [SM] + [VM] * 5,
        limit=4,
    )
    tod, tev = swap(t_od, t_ev, "gx")
    (out,) = call(
        bind(fourth_kernel),
        [(rows, cols, depth)],
        [meta, currents, gci, gco, base, e3, rod, rev, tod, tev, vod, vev, wts, scl, two, hwts,
         hscl, htwo],
        [SM] * 2 + [VM] * 16,
        scratch=vmem((n + 2, ext, LANES), wide(rows + 4), wide(rows + 2),
                     (rows, cols, depth))
        + [pltpu.SemaphoreType.DMA((rows,))],
        out_specs=[hbm],
        limit=13,
    )
    return out


def solution(mesh):
    tiled = P("gx", "gy", None)
    return jax.shard_map(
        per_device,
        mesh=mesh,
        in_specs=(tiled, tiled, P(), P(), P(), P(), P()),
        out_specs=tiled,
        check_vma=False,
    )
```

time: 72.5 us -> 68.4 us (0.943)
  waiting for transfers between devices: 13.1 us -> 9.56 us
  local copies, waits for them, and re-layouts: 3.9 us -> 1.71 us
  starting transfers between devices: 20.4 us -> 22.1 us
    ppermute x6, waiting for transfers between devices: 12.8 us -> 9.44 us  [swap(): lax.ppermute(od, axis, odd_pairs)]
    unnamed x18 -> x14, local copies, waits for them, and re-layouts: 3.82 us -> 1.62 us
    ppermute x6, starting transfers between devices: 18.5 us -> 20 us  [swap(): lax.ppermute(od, axis, odd_pairs)]
    pallas_call x9 -> x11, Pallas kernels: 34.2 us -> 33.5 us  [call(): pl.pallas_call(kernel, out_shape=[jax.ShapeDtypeStruct(shape, F32) for sh...]
  transfers between devices with their start and end apart: 12 -> 12, of which waited for: 6 -> 5; matrix products, arithmetic and copies ran while one was open for 0% -> 0% of each run, Pallas kernels for 26% -> 32%
where the time goes in v2:
time: 68.4 us; the launch traced here: 67.4 us
  Pallas kernels  33.5 us (49%)
  starting transfers between devices  22.1 us (32%)
  waiting for transfers between devices  9.56 us (14%)
  local copies, waits for them, and re-layouts  1.71 us (2%)
    pallas_call x11, Pallas kernels, call(): pl.pallas_call(kernel, out_shape=[jax.ShapeDtypeStruct(shape, F32) for sh...  33.5 us
    ppermute x6, starting transfers between devices, swap(): lax.ppermute(od, axis, odd_pairs)  20 us
    ppermute x6, waiting for transfers between devices, swap(): lax.ppermute(od, axis, odd_pairs)  9.44 us
    ppermute x6, starting transfers between devices, swap(): lax.ppermute(ev, axis, even_pairs)  2.07 us
    unnamed x14, local copies, waits for them, and re-layouts  1.62 us
  transfers between devices with their start and end apart: 12, of which 5 were waited for; matrix products, arithmetic and copies ran while one was open for 0% of the time, Pallas kernels for 32%

profile of v2, /device:TPU:11, one launch (start us, length us, event | category | flops | bytes accessed | tf_op | source)
XLA Modules:
  0.0 67.4 jit_solution(14435424538531609966)
XLA Ops:
  0.0 2.2 %shard_map.78 = f32[4,256,256]{2,1,0:T(8,128)} custom-call(f32[8,256,256]{2,1,0:T(8,128)} %pot.9, s32[8,256,256]{2,1,0:T(8,128)} %cls.9), custom_call_target="tpu_custom_call" | custom-call | flops 1 | bytes 1 | tf_op jit(solution)/shard_map/pallas_call | solution.py:727
  2.2 3.7 %collective-permute-start.4 = (f32[4,256,256]{2,1,0:T(8,128)}, f32[4,256,256]{2,1,0:T(8,128)}, u32[]{:S(2)}, u32[]{:S(2)}) collective-permute-start(f32[4,256,256]{2,1,0:T(8,128)} %shard_map.78), channel_id=1, source_target_pairs={{4,8},{8,4},{12,16},{16,12},{20,24},{24,20},{5,9},{9,5},{13,17},{1... | collective-permute-start | bytes 3145736 | tf_op jit(solution)/shard_map/ppermute | solution.py:751
  5.9 2.2 %shard_map.79 = f32[4,256,256]{2,1,0:T(8,128)} custom-call(f32[8,256,256]{2,1,0:T(8,128)} %pot.9, s32[8,256,256]{2,1,0:T(8,128)} %cls.9), custom_call_target="tpu_custom_call" | custom-call | flops 1 | bytes 1 | tf_op jit(solution)/shard_map/pallas_call | solution.py:727
  8.1 0.1 collective-permute-start.5
  8.2 1.7 %shard_map.73 = f32[2,8,16,256]{3,2,1,0:T(8,128)} custom-call(f32[8,256,256]{2,1,0:T(8,128)} %pot.9, s32[8,256,256]{2,1,0:T(8,128)} %cls.9), custom_call_target="tpu_custom_call" | custom-call | flops 1 | bytes 1 | tf_op jit(solution)/shard_map/pallas_call | solution.py:727
  9.9 0.0 copy-start.3
  9.9 0.0 copy-start.4
  9.9 0.0 copy-start.5
  9.9 0.0 copy-start.6
  9.9 0.0 copy-start
  9.9 0.0 copy-start.2
  10.0 3.3 %collective-permute-start = (f32[2,8,16,256]{3,2,1,0:T(8,128)}, f32[2,8,16,256]{3,2,1,0:T(8,128)S(1)}, u32[]{:S(2)}, u32[]{:S(2)}) collective-permute-start(f32[2,8,16,256]{3,2,1,0:T(8,128)} %shard_map.73), channel_id=1, source_target_pairs={{1,2},{2,1},{5,6},{6,5},{9,10},{10,9},{13,14},{14,13},{17,18},{18,... | collective-permute-start | bytes 786440 | tf_op jit(solution)/shard_map/ppermute | solution.py:751
  13.3 1.7 %shard_map.74 = f32[2,8,16,256]{3,2,1,0:T(8,128)} custom-call(f32[8,256,256]{2,1,0:T(8,128)} %pot.9, s32[8,256,256]{2,1,0:T(8,128)} %cls.9), custom_call_target="tpu_custom_call" | custom-call | flops 1 | bytes 1 | tf_op jit(solution)/shard_map/pallas_call | solution.py:727
  15.0 0.1 collective-permute-start.1
  15.1 0.0 copy-done.3
  15.1 0.0 copy-done.4
  15.1 0.0 copy-done.5
  15.2 0.1 concatenate.3.meta
  15.2 0.0 copy-done.6
  15.3 0.0 copy-start.1
  15.3 1.6 %copy-done.1 = s32[8,256,256]{2,1,0:T(8,128)S(1)} copy-done((s32[8,256,256]{2,1,0:T(8,128)S(1)}, s32[8,256,256]{2,1,0:T(8,128)}, u32[]{:S(2)}) %copy-start.1) | copy-done | bytes 2097176
  16.9 5.4 %shard_map.75 = (f32[4,2,304,128]{3,2,1,0:T(8,128)S(1)}, f32[4,2,304,128]{3,2,1,0:T(8,128)S(1)}, f32[2,2,288,128]{3,2,1,0:T(8,128)S(1)}, f32[2,2,304,128]{3,2,1,...) custom-call(s32[8]{0:T(128)S(1)} %concatenate.3.meta, ...), custom_call_target="tpu_custom_call" | custom-call | flops 1 | bytes 1 | tf_op jit(solution)/shard_map/pallas_call | solution.py:727
  22.3 0.0 collective-permute-done.yod
  22.3 0.1 collective-permute-done.1.yev
  22.4 1.5 %shard_map.76 = (f32[4,2,304,128]{3,2,1,0:T(8,128)S(1)}, f32[4,2,304,128]{3,2,1,0:T(8,128)S(1)}, f32[2,2,288,128]{3,2,1,0:T(8,128)S(1)}, f32[2,2,304,128]{3,2,1,...) custom-call(s32[8]{0:T(128)S(1)} %concatenate.3.meta, ...), custom_call_target="tpu_custom_call", output_to_operand_aliasing={{0}: (5, {}), {1}: (6, {}), {2}: (7, {}), {3}: (8, {}), {4}... | custom-call | flops 1 | bytes 1 | tf_op jit(solution)/shard_map/pallas_call | solution.py:727
  23.9 1.7 %collective-permute-start.3 = (f32[768,128]{1,0:T(8,128)S(1)}, f32[768,128]{1,0:T(8,128)S(1)}, u32[]{:S(2)}, u32[]{:S(2)}) collective-permute-start(f32[768,128]{1,0:T(8,128)S(1)} %get-tuple-element.88), channel_id=1, source_target_pairs={{0,4},{4,0},{8,12},{12,8},{16,20},{20,16},{24,28},{28,24},{1,5},{5... | collective-permute-start | bytes 1179656 | tf_op jit(solution)/shard_map/ppermute | solution.py:751
  25.6 3.0 %collective-permute-start.2 = (f32[768,128]{1,0:T(8,128)S(1)}, f32[768,128]{1,0:T(8,128)S(1)}, u32[]{:S(2)}, u32[]{:S(2)}) collective-permute-start(f32[768,128]{1,0:T(8,128)S(1)} %get-tuple-element.86.refs_13_), channel_id=1, source_target_pairs={{4,8},{8,4},{12,16},{16,12},{20,24},{24,20},{5,9},{9,5},{13,17},{1... | collective-permute-start | bytes 1179656 | tf_op jit(solution)/shard_map/ppermute | solution.py:751
  28.6 2.3 %shard_map.77 = (f32[4,2,304,128]{3,2,1,0:T(8,128)S(1)}, f32[2,2,288,128]{3,2,1,0:T(8,128)S(1)}, f32[8,144,128]{2,1,0:T(8,128)S(1)}, f32[7,2,144,128]{3,2,1,0:T(8,128)S(1)}, f32[4,144,128]{2,1,0:T(8,128)S(1)}) custom-call(s32[8]{0:T(128)S(1)} %concatenate.3.meta, f32[2]{0:T(128)S(1)} %copy-done.2, f32[4,2,304,128]{3,2,1,0:T(8,128)S(1)} %get-tuple-element.73.refs_0_.res, ...), custom_call_target="tpu_custom_call" | custom-call | flops 1 | bytes 1 | tf_op jit(solution)/shard_map/pallas_call | solution.py:727
  30.9 0.0 collective-permute-done.4.xod
  30.9 0.0 collective-permute-done.5.xev
  30.9 5.8 %shard_map.80 = (f32[4,2,304,128]{3,2,1,0:T(8,128)S(1)}, f32[4,2,304,128]{3,2,1,0:T(8,128)S(1)}, f32[4,2,288,128]{3,2,1,0:T(8,128)S(1)}, f32[2,2,304,128]{3,2,1,...) custom-call(s32[8]{0:T(128)S(1)} %concatenate.3.meta, ...), custom_call_target="tpu_custom_call" | custom-call | flops 1 | bytes 1 | tf_op jit(solution)/shard_map/pallas_call | solution.py:727
  36.8 0.0 collective-permute-done.3.sev
  36.8 2.3 %collective-permute-done.2.sod = f32[768,128]{1,0:T(8,128)S(1)} collective-permute-done((f32[768,128]{1,0:T(8,128)S(1)}, f32[768,128]{1,0:T(8,128)S(1)}, u32[]{:S(2)}, u32[]{:S(2)}) %collective-permute-start.2) | collective-permute-done | bytes 393248 | tf_op jit(solution)/shard_map/ppermute | solution.py:751
  39.1 2.7 %shard_map.81 = (f32[4,2,304,128]{3,2,1,0:T(8,128)S(1)}, f32[4,2,304,128]{3,2,1,0:T(8,128)S(1)}, f32[4,2,288,128]{3,2,1,0:T(8,128)S(1)}, f32[2,2,304,128]{3,2,1,...) custom-call(s32[8]{0:T(128)S(1)} %concatenate.3.meta, ...), custom_call_target="tpu_custom_call", output_to_operand_aliasing={{0}: (17, {}), {1}: (18, {}), {2}: (19, {}), {3}: (20, {}),... | custom-call | flops 1 | bytes 1 | tf_op jit(solution)/shard_map/pallas_call | solution.py:727
  41.8 3.4 %collective-permute-start.6 = (f32[3,144,128]{2,1,0:T(8,128)S(1)}, f32[3,144,128]{2,1,0:T(8,128)S(1)}, u32[]{:S(2)}, u32[]{:S(2)}) collective-permute-start(f32[3,144,128]{2,1,0:T(8,128)S(1)} %get-tuple-element.105), channel_id=1, source_target_pairs={{4,8},{8,4},{12,16},{16,12},{20,24},{24,20},{5,9},{9,5},{13,17},{1... | collective-permute-start | bytes 663560 | tf_op jit(solution)/shard_map/ppermute | solution.py:751
  45.2 0.1 collective-permute-start.7
  45.3 3.0 %collective-permute-start.10 = (f32[2,288,128]{2,1,0:T(8,128)S(1)}, f32[2,288,128]{2,1,0:T(8,128)S(1)}, u32[]{:S(2)}, u32[]{:S(2)}) collective-permute-start(f32[2,288,128]{2,1,0:T(8,128)S(1)} %get-tuple-element.110), channel_id=1, source_target_pairs={{4,8},{8,4},{12,16},{16,12},{20,24},{24,20},{5,9},{9,5},{13,17},{1... | collective-permute-start | bytes 884744 | tf_op jit(solution)/shard_map/ppermute | solution.py:751
  48.3 0.1 collective-permute-start.11
  48.4 3.4 %collective-permute-done.6.rod = f32[3,144,128]{2,1,0:T(8,128)S(1)} collective-permute-done((f32[3,144,128]{2,1,0:T(8,128)S(1)}, f32[3,144,128]{2,1,0:T(8,128)S(1)}, u32[]{:S(2)}, u32[]{:S(2)}) %collective-permute-start.6) | collective-permute-done | bytes 221216 | tf_op jit(solution)/shard_map/ppermute | solution.py:751
  51.8 0.0 collective-permute-done.7.rev
  51.8 1.2 %shard_map.82 = (f32[4,144,128]{2,1,0:T(8,128)S(1)}, f32[2,144,128]{2,1,0:T(8,128)S(1)}, f32[2,144,128]{2,1,0:T(8,128)S(1)}) custom-call(s32[8]{0:T(128)S(1)} %concatenate.3.meta, f32[7,2,144,128]{3,2,1,0:T(8,128)S(1)} %get-tuple-element.87.gci, f32[6,2,144,128]{3,2,1,0:T(8,128)S(1)} %get-tuple-element.103.gco, f32[4,144,128]{2,1,0:T(8,128)S(1)} %get-tuple-element.104.base, ...), custom_call_target="tpu_custom_call" | custom-call | flops 1 | bytes 1 | tf_op jit(solution)/shard_map/pallas_call | solution.py:727
  53.0 3.5 %collective-permute-start.8 = (f32[2,144,128]{2,1,0:T(8,128)S(1)}, f32[2,144,128]{2,1,0:T(8,128)S(1)}, u32[]{:S(2)}, u32[]{:S(2)}) collective-permute-start(f32[2,144,128]{2,1,0:T(8,128)S(1)} %get-tuple-element.108), channel_id=1, source_target_pairs={{4,8},{8,4},{12,16},{16,12},{20,24},{24,20},{5,9},{9,5},{13,17},{1... | collective-permute-start | bytes 442376 | tf_op jit(solution)/shard_map/ppermute | solution.py:751
  56.6 0.1 collective-permute-start.9
  56.6 1.5 %collective-permute-done.10.vod = f32[2,288,128]{2,1,0:T(8,128)S(1)} collective-permute-done((f32[2,288,128]{2,1,0:T(8,128)S(1)}, f32[2,288,128]{2,1,0:T(8,128)S(1)}, u32[]{:S(2)}, u32[]{:S(2)}) %collective-permute-start.10) | collective-permute-done | bytes 294944 | tf_op jit(solution)/shard_map/ppermute | solution.py:751
  58.1 0.0 collective-permute-done.11.vev
  58.1 2.2 %collective-permute-done.8.tod = f32[2,144,128]{2,1,0:T(8,128)S(1)} collective-permute-done((f32[2,144,128]{2,1,0:T(8,128)S(1)}, f32[2,144,128]{2,1,0:T(8,128)S(1)}, u32[]{:S(2)}, u32[]{:S(2)}) %collective-permute-start.8) | collective-permute-done | bytes 147488 | tf_op jit(solution)/shard_map/ppermute | solution.py:751
  60.4 0.0 collective-permute-done.9.tev
  60.4 6.9 %shard_map.83 = f32[8,256,256]{2,1,0:T(8,128)} custom-call(s32[8]{0:T(128)S(1)} %concatenate.3.meta, f32[2]{0:T(128)S(1)} %copy-done.2, f32[7,2,144,128]{3,2,1,0:T(8,128)S(1)} %get-tuple-element.87.gci, f32[6,2,144,128]{3,2,1,0:T(8,128)S(1)} %get-tuple-element.103.gco, f32[4,144,128]{2,1,0:T(8,128)S(1)} %get-tuple-element.104.base, ...), custom_call_target="tpu_custom_call" | custom-call | flops 1 | bytes 1 | tf_op jit(solution)/shard_map/pallas_call | solution.py:727
  (4 shorter events, 0.0 us)
Async XLA Ops:
  2.2 28.7 %collective-permute-start.4 = (f32[4,256,256]{2,1,0:T(8,128)}, f32[4,256,256]{2,1,0:T(8,128)}, u32[]{:S(2)}, u32[]{:S(2)}) collective-permute-start(f32[4,256,256]{2,1,0:T(8,128)} %shard_map.78), channel_id=1, source_target_pairs={{4,8},{8,4},{12,16},{16,12},{20,24},{24,20},{5,9},{9,5},{13,17},{1... | collective-permute-start | bytes 3145736 | tf_op jit(solution)/shard_map/ppermute | solution.py:751
  8.1 22.8 %collective-permute-start.5 = (f32[4,256,256]{2,1,0:T(8,128)}, f32[4,256,256]{2,1,0:T(8,128)}, u32[]{:S(2)}, u32[]{:S(2)}) collective-permute-start(f32[4,256,256]{2,1,0:T(8,128)} %shard_map.79), channel_id=1, source_target_pairs={{0,4},{4,0},{8,12},{12,8},{16,20},{20,16},{24,28},{28,24},{1,5},{5... | collective-permute-start | bytes 3145736 | tf_op jit(solution)/shard_map/ppermute | solution.py:751
  9.9 5.2 %copy-start.3 = (s32[2]{0:T(128)S(1)}, s32[2]{0:T(128)}, u32[]{:S(2)}) copy-start(s32[2]{0:T(128)} %param.11) | copy-start | bytes 28
  9.9 5.2 %copy-start.4 = (s32[2]{0:T(128)S(1)}, s32[2]{0:T(128)}, u32[]{:S(2)}) copy-start(s32[2]{0:T(128)} %param.10) | copy-start | bytes 28
  9.9 5.2 %copy-start.5 = (s32[2]{0:T(128)S(1)}, s32[2]{0:T(128)}, u32[]{:S(2)}) copy-start(s32[2]{0:T(128)} %param.12) | copy-start | bytes 28
  9.9 5.3 %copy-start.6 = (f32[8]{0:T(128)S(1)}, f32[8]{0:T(128)}, u32[]{:S(2)}) copy-start(f32[8]{0:T(128)} %param.9) | copy-start | bytes 100
  9.9 5.3 %copy-start = (f32[8,256,256]{2,1,0:T(8,128)S(1)}, f32[8,256,256]{2,1,0:T(8,128)}, u32[]{:S(2)}) copy-start(f32[8,256,256]{2,1,0:T(8,128)} %pot.9) | copy-start | bytes 6291460
  9.9 5.3 %copy-start.2 = (f32[2]{0:T(128)S(1)}, f32[2]{0:T(128)}, u32[]{:S(2)}) copy-start(f32[2]{0:T(128)} %cur.11) | copy-start | bytes 28
  10.0 12.3 %collective-permute-start = (f32[2,8,16,256]{3,2,1,0:T(8,128)}, f32[2,8,16,256]{3,2,1,0:T(8,128)S(1)}, u32[]{:S(2)}, u32[]{:S(2)}) collective-permute-start(f32[2,8,16,256]{3,2,1,0:T(8,128)} %shard_map.73), channel_id=1, source_target_pairs={{1,2},{2,1},{5,6},{6,5},{9,10},{10,9},{13,14},{14,13},{17,18},{18,... | collective-permute-start | bytes 786440 | tf_op jit(solution)/shard_map/ppermute | solution.py:751
  15.0 7.4 %collective-permute-start.1 = (f32[2,8,16,256]{3,2,1,0:T(8,128)}, f32[2,8,16,256]{3,2,1,0:T(8,128)S(1)}, u32[]{:S(2)}, u32[]{:S(2)}) collective-permute-start(f32[2,8,16,256]{3,2,1,0:T(8,128)} %shard_map.74), channel_id=1, source_target_pairs={{0,1},{1,0},{2,3},{3,2},{4,5},{5,4},{6,7},{7,6},{8,9},{9,8},{10,11... | collective-permute-start | bytes 786440 | tf_op jit(solution)/shard_map/ppermute | solution.py:751
  15.3 1.6 %copy-start.1 = (s32[8,256,256]{2,1,0:T(8,128)S(1)}, s32[8,256,256]{2,1,0:T(8,128)}, u32[]{:S(2)}) copy-start(s32[8,256,256]{2,1,0:T(8,128)} %cls.9) | copy-start | bytes 6291460
  23.9 12.9 %collective-permute-start.3 = (f32[768,128]{1,0:T(8,128)S(1)}, f32[768,128]{1,0:T(8,128)S(1)}, u32[]{:S(2)}, u32[]{:S(2)}) collective-permute-start(f32[768,128]{1,0:T(8,128)S(1)} %get-tuple-element.88), channel_id=1, source_target_pairs={{0,4},{4,0},{8,12},{12,8},{16,20},{20,16},{24,28},{28,24},{1,5},{5... | collective-permute-start | bytes 1179656 | tf_op jit(solution)/shard_map/ppermute | solution.py:751
  25.6 13.5 %collective-permute-start.2 = (f32[768,128]{1,0:T(8,128)S(1)}, f32[768,128]{1,0:T(8,128)S(1)}, u32[]{:S(2)}, u32[]{:S(2)}) collective-permute-start(f32[768,128]{1,0:T(8,128)S(1)} %get-tuple-element.86.refs_13_), channel_id=1, source_target_pairs={{4,8},{8,4},{12,16},{16,12},{20,24},{24,20},{5,9},{9,5},{13,17},{1... | collective-permute-start | bytes 1179656 | tf_op jit(solution)/shard_map/ppermute | solution.py:751
  41.8 10.0 %collective-permute-start.6 = (f32[3,144,128]{2,1,0:T(8,128)S(1)}, f32[3,144,128]{2,1,0:T(8,128)S(1)}, u32[]{:S(2)}, u32[]{:S(2)}) collective-permute-start(f32[3,144,128]{2,1,0:T(8,128)S(1)} %get-tuple-element.105), channel_id=1, source_target_pairs={{4,8},{8,4},{12,16},{16,12},{20,24},{24,20},{5,9},{9,5},{13,17},{1... | collective-permute-start | bytes 663560 | tf_op jit(solution)/shard_map/ppermute | solution.py:751
  45.2 6.6 %collective-permute-start.7 = (f32[3,144,128]{2,1,0:T(8,128)S(1)}, f32[3,144,128]{2,1,0:T(8,128)S(1)}, u32[]{:S(2)}, u32[]{:S(2)}) collective-permute-start(f32[3,144,128]{2,1,0:T(8,128)S(1)} %get-tuple-element.106), channel_id=1, source_target_pairs={{0,4},{4,0},{8,12},{12,8},{16,20},{20,16},{24,28},{28,24},{1,5},{5... | collective-permute-start | bytes 663560 | tf_op jit(solution)/shard_map/ppermute | solution.py:751
  45.3 12.8 %collective-permute-start.10 = (f32[2,288,128]{2,1,0:T(8,128)S(1)}, f32[2,288,128]{2,1,0:T(8,128)S(1)}, u32[]{:S(2)}, u32[]{:S(2)}) collective-permute-start(f32[2,288,128]{2,1,0:T(8,128)S(1)} %get-tuple-element.110), channel_id=1, source_target_pairs={{4,8},{8,4},{12,16},{16,12},{20,24},{24,20},{5,9},{9,5},{13,17},{1... | collective-permute-start | bytes 884744 | tf_op jit(solution)/shard_map/ppermute | solution.py:751
  48.3 9.8 %collective-permute-start.11 = (f32[2,288,128]{2,1,0:T(8,128)S(1)}, f32[2,288,128]{2,1,0:T(8,128)S(1)}, u32[]{:S(2)}, u32[]{:S(2)}) collective-permute-start(f32[2,288,128]{2,1,0:T(8,128)S(1)} %get-tuple-element.111), channel_id=1, source_target_pairs={{0,4},{4,0},{8,12},{12,8},{16,20},{20,16},{24,28},{28,24},{1,5},{5... | collective-permute-start | bytes 884744 | tf_op jit(solution)/shard_map/ppermute | solution.py:751
  53.0 7.4 %collective-permute-start.8 = (f32[2,144,128]{2,1,0:T(8,128)S(1)}, f32[2,144,128]{2,1,0:T(8,128)S(1)}, u32[]{:S(2)}, u32[]{:S(2)}) collective-permute-start(f32[2,144,128]{2,1,0:T(8,128)S(1)} %get-tuple-element.108), channel_id=1, source_target_pairs={{4,8},{8,4},{12,16},{16,12},{20,24},{24,20},{5,9},{9,5},{13,17},{1... | collective-permute-start | bytes 442376 | tf_op jit(solution)/shard_map/ppermute | solution.py:751
  56.6 3.8 %collective-permute-start.9 = (f32[2,144,128]{2,1,0:T(8,128)S(1)}, f32[2,144,128]{2,1,0:T(8,128)S(1)}, u32[]{:S(2)}, u32[]{:S(2)}) collective-permute-start(f32[2,144,128]{2,1,0:T(8,128)S(1)} %get-tuple-element.109), channel_id=1, source_target_pairs={{0,4},{4,0},{8,12},{12,8},{16,20},{20,16},{24,28},{28,24},{1,5},{5... | collective-permute-start | bytes 442376 | tf_op jit(solution)/shard_map/ppermute | solution.py:751
